TPU v7x, 128 devices: a whole 4x4x4 slice. The times are simulated.
128 devices in a mesh: gx: 8 (over y, core), gy: 4 (over x), gz: 4 (over z).
Axes of the slice: x: 4, y: 4, z: 4, core: 2. Of those that a mesh axis runs over, the one named last changes fastest.
Arguments:
- pressure_source: float32 [128, 256, 1024], P('gx', 'gy', 'gz'), may hold values from -6 to 6
- cell_density: float32 [1024], P('gz'), may hold values from 0.3 to 3
- face_density: float32 [1024], P('gz'), may hold values from 0.3 to 3
Outputs:
- smoothed: float32 [128, 256, 1024], P('gx', 'gy', 'gz')
- coarse_solution: float32 [16, 32, 128], P('gx')
All inputs are finite; a program needn't handle non-finite values.
Results may differ from a plain program's by a relative error of at most 0.0001.
Values sent between devices are 32-bit elements; how exact they have to be, the bound alone decides.
A program may use at most 192 MiB of HBM per device.

v0:
```python
import jax
import jax.numpy as jnp
from jax import lax
from jax.sharding import PartitionSpec as P

LEVELS = 3
SWEEPS = 6
COARSE_SWEEPS = 8


damping = 0.8


def padded_2(block, sides, width):
    for axis, dim in sides:
        count = lax.axis_size(axis)
        forward = [(i, i + 1) for i in range(count - 1)]
        forward.append((count - 1, 0))
        backward = [(target, source) for source, target in forward]
        low = lax.ppermute(
            lax.slice_in_dim(block, block.shape[dim] - width, None, axis=dim), axis, forward
        )
        high = lax.ppermute(lax.slice_in_dim(block, 0, width, axis=dim), axis, backward)
        block = jnp.concatenate([low, block, high], axis=dim)
    return block


def passed_along(block, axis, distance):
    devices = range(lax.axis_size(axis))
    route = [((i - distance) % len(devices), i) for i in devices]
    return lax.ppermute(block, axis, route)


def from_behind(value, axis, steps):
    count = lax.axis_size(axis)
    leading, last = (max(0, -steps), min(count, count - steps))
    return lax.ppermute(value, axis, [(source, source + steps) for source in range(leading, last)])


def level_apply(iterate, centre_coef, below_coef, above_coef, bottom_flag):
    padded = padded_2(iterate, (("gx", 0), ("gy", 1), ("gz", 2)), 1)
    horizontal = (
        4.0 * iterate
        - padded[:-2, 1:-1, 1:-1]
        - padded[2:, 1:-1, 1:-1]
        - padded[1:-1, :-2, 1:-1]
        - padded[1:-1, 2:, 1:-1]
    )
    depth = iterate.shape[2]
    first_plane = lax.broadcasted_iota(jnp.int32, (1, 1, depth), 2) == 0
    beneath = jnp.where(first_plane & bottom_flag, 0.0, padded[1:-1, 1:-1, :-2])
    overhead = padded[1:-1, 1:-1, 2:]
    return (
        centre_coef * horizontal
        + below_coef * (iterate - beneath)
        + above_coef * (iterate - overhead)
    )


def slab_apply(iterate, centre_coef, below_coef, above_coef):
    from_west = passed_along(iterate[-1:], "gx", 1)
    from_east = passed_along(iterate[:1], "gx", -1)
    western = jnp.concatenate([from_west, iterate[:-1]], axis=0)
    eastern = jnp.concatenate([iterate[1:], from_east], axis=0)
    horizontal = (
        4.0 * iterate - western - eastern - jnp.roll(iterate, 1, 1) - jnp.roll(iterate, -1, 1)
    )
    zero_plane = jnp.zeros_like(iterate[:, :, :1])
    beneath = jnp.concatenate([zero_plane, iterate[:, :, :-1]], axis=2)
    overhead = jnp.concatenate([iterate[:, :, 1:], zero_plane], axis=2)
    return (
        centre_coef * horizontal
        + below_coef * (iterate - beneath)
        + above_coef * (iterate - overhead)
    )


def smooth_with(operator, source_term, centre_coef, below_coef, above_coef, sweep_count):
    inverse_diag = 1.0 / (4.0 * centre_coef + below_coef + above_coef)
    iterate = damping * source_term * inverse_diag
    for sweep_index in range(sweep_count - 1):
        iterate = iterate + damping * (source_term - operator(iterate)) * inverse_diag
    return iterate


def restrict(residual):
    extent = residual.shape
    blocks = residual.reshape(extent[0] // 2, 2, extent[1] // 2, 2, extent[2] // 2, 2)
    return 0.5 * jnp.sum(blocks, axis=(1, 3, 5))


def on_device(pressure_source, cell_density, face_density):
    bottom_flag = lax.axis_index("gz") == 0
    top_value = from_behind(face_density[:1], "gz", -1)
    centre_coef = cell_density
    below_coef = face_density
    above_coef = jnp.concatenate([face_density[1:], top_value])
    source_term = pressure_source
    smoothed = pressure_source
    for level_index in range(LEVELS):

        def operator(
            iterate, centre_coef=centre_coef, below_coef=below_coef, above_coef=above_coef
        ):
            return level_apply(iterate, centre_coef, below_coef, above_coef, bottom_flag)

        iterate = smooth_with(operator, source_term, centre_coef, below_coef, above_coef, SWEEPS)
        residual = source_term - operator(iterate)
        if level_index == 0:
            smoothed = iterate
        source_term = restrict(residual)
        centre_coef = 0.5 * (centre_coef[0::2] + centre_coef[1::2])
        below_coef = below_coef[0::2]
        above_coef = above_coef[1::2]
    columns = lax.all_gather(source_term, "gy", axis=1, tiled=True)
    slab_source, slab_centre, slab_below, slab_above = (
        lax.all_gather(columns, "gz", axis=2, tiled=True),
        lax.all_gather(centre_coef, "gz", axis=0, tiled=True),
        lax.all_gather(below_coef, "gz", axis=0, tiled=True),
        lax.all_gather(above_coef, "gz", axis=0, tiled=True),
    )

    def coarse_operator(iterate):
        return slab_apply(iterate, slab_centre, slab_below, slab_above)

    coarse_solution = smooth_with(
        coarse_operator, slab_source, slab_centre, slab_below, slab_above, COARSE_SWEEPS
    )
    return (smoothed, coarse_solution)


def solution(mesh):
    return jax.shard_map(
        on_device,
        mesh=mesh,
        in_specs=(P("gx", "gy", "gz"), P("gz"), P("gz")),
        out_specs=(P("gx", "gy", "gz"), P("gx", None, None)),
        check_vma=False,
    )
```

profile of v0, /device:TPU:57, one launch (start us, length us, event | category | flops | bytes accessed | tf_op | source)
XLA Modules:
  0.0 528.1 jit_solution(14697296491463403184)
XLA Ops:
  12.5 3.6 collective-permute-done.2
  28.5 4.5 fusion.78
  36.9 3.6 collective-permute-done.8
  52.1 4.4 fusion.63
  60.4 3.6 collective-permute-done.14
  76.2 4.2 fusion.48
  83.9 3.6 collective-permute-done.20
  99.3 4.5 fusion.33
  107.4 3.6 collective-permute-done.26
  123.8 4.4 fusion.18
  132.2 3.6 collective-permute-done.32
  148.0 4.4 fusion.3
  152.4 68.4 %reshape.50 = f32[8,2,32,2,128,2]{5,4,3,2,1,0:T(8,128)} reshape(f32[16,64,256]{2,1,0:T(8,128)S(1)} %fusion.3) | data formatting | bytes 2097152 | tf_op jit(solution)/shard_map/reshape | solution.py:88
  220.8 20.8 %reduce_sum.27 = f32[8,32,128]{2,1,0:T(8,128)S(1)} reduce(f32[8,2,32,2,128,2]{5,4,3,2,1,0:T(8,128)} %reshape.50, f32[]{:T(128)} %constant.14.clone.1), dimensions={1,3,5}, to_apply=%region_0.1 | reduce | flops 229376 | bytes 1179652 | tf_op jit(solution)/shard_map/reduce_sum | solution.py:89
  244.8 3.5 collective-permute-done.38
  254.7 4.0 collective-permute-done.41
  262.8 3.5 collective-permute-done.44
  272.0 3.9 collective-permute-done.47
  280.7 3.5 collective-permute-done.50
  290.1 3.9 collective-permute-done.53
  298.5 3.5 collective-permute-done.56
  307.6 4.2 collective-permute-done.59
  315.7 3.5 collective-permute-done.62
  324.8 4.3 collective-permute-done.65
  333.0 3.5 collective-permute-done.68
  341.9 3.9 collective-permute-done.71
  347.2 9.7 %reshape.51 = f32[4,2,16,2,64,2]{5,4,3,2,1,0:T(8,128)} reshape(f32[8,32,128]{2,1,0:T(8,128)S(1)} %fusion.91) | data formatting | bytes 262144 | tf_op jit(solution)/shard_map/reshape | solution.py:88
  357.0 4.0 reduce_sum.28
  363.5 3.5 collective-permute-done.74
  379.7 3.5 collective-permute-done.80
  395.0 3.5 collective-permute-done.86
  406.9 2.9 collective-permute-start.91
  410.7 3.5 collective-permute-done.92
  426.1 3.5 collective-permute-done.98
  429.6 2.9 collective-permute-start.100
  433.3 2.9 collective-permute-done.99
  441.4 2.9 collective-permute-start.103
  451.8 6.4 %all-reduce.17 = (f32[128]{0:T(128)S(1)}, f32[128]{0:T(128)S(1)}, f32[128]{0:T(128)S(1)}) all-reduce(f32[128]{0:T(128)S(1)} %dynamic-update-slice.2, f32[128]{0:T(128)S(1)} %dynamic-update-slice.1, f32[128]{0:T(128)S(1)} %multiply_dynamic-update-slice_fusion), channel_id=1, replica_groups=mesh['gx'=8,'gy'=4,'gz'=4] {'gz'}, use_global_device_ids=true, to_apply=%add.16 | all-reduce | flops 384 | bytes 3072
  464.9 9.0 %all_gather.15 = f32[2,32,32]{2,0,1:T(2,128)S(1)} all-gather(f32[2,8,32]{2,0,1:T(2,128)S(1)} %copy.355), channel_id=1, replica_groups=mesh['gx'=8,'gy'=4,'gz'=4] {'gy'}, dimensions={1}, use_global_device_ids=true | all-gather | bytes 10240 | tf_op jit(solution)/shard_map/all_gather | solution.py:115
  474.0 12.1 %all_gather.16 = f32[2,32,128]{1,0,2:T(2,128)S(1)} all-gather(f32[2,32,32]{1,0,2:T(2,128)S(1)} %copy.356), channel_id=1, replica_groups=mesh['gx'=8,'gy'=4,'gz'=4] {'gz'}, dimensions={2}, use_global_device_ids=true | all-gather | bytes 40960 | tf_op jit(solution)/shard_map/all_gather | solution.py:117
  486.3 8.9 %collective-permute-start.109 = (f32[1,32,128]{2,1,0:T(8,128)S(1)}, f32[1,32,128]{2,1,0:T(8,128)S(1)}, u32[]{:S(2)}, u32[]{:S(2)}) collective-permute-start(f32[1,32,128]{2,1,0:T(8,128)S(1)} %get-tuple-element.167), channel_id=1, source_target_pairs={{112,0},{0,16},{16,32},{32,48},{48,64},{64,80},{80,96},{96,112},{1... | collective-permute-start | bytes 49160 | tf_op jit(solution)/shard_map/ppermute | solution.py:31
  496.0 3.5 collective-permute-done.110
  500.9 3.2 collective-permute-done.112
  505.5 3.2 collective-permute-done.114
  510.1 3.2 collective-permute-done.116
  514.7 3.2 collective-permute-done.118
  519.3 3.2 collective-permute-done.120
  523.9 3.2 collective-permute-done.122
  (498 shorter events, 241.2 us)
Async XLA Ops:
  1.8 4.7 collective-permute-start
  11.2 4.9 collective-permute-start.2
  35.6 4.9 collective-permute-start.8
  59.1 4.9 collective-permute-start.14
  64.1 4.2 collective-permute-start.15
  82.5 4.9 collective-permute-start.20
  106.1 4.9 collective-permute-start.26
  111.0 4.2 collective-permute-start.27
  128.3 4.0 collective-permute-start.31
  130.9 4.9 collective-permute-start.32
  135.8 4.0 collective-permute-start.33
  243.9 4.4 collective-permute-start.38
  252.4 6.2 %collective-permute-start.41 = (f32[10,34,1]{2,1,0:T(8,128)S(1)}, f32[10,34,1]{2,1,0:T(8,128)S(1)}, u32[]{:S(2)}, u32[]{:S(2)}) collective-permute-start(f32[10,34,1]{2,1,0:T(8,128)S(1)} %get-tuple-element.63), channel_id=1, source_target_pairs={{0,1},{1,2},{2,3},{3,0},{4,5},{5,6},{6,7},{7,4},{8,9},{9,10},{10,1... | collective-permute-start | bytes 4088 | tf_op jit(solution)/shard_map/ppermute | solution.py:20
  254.2 5.8 %collective-permute-start.42 = (f32[10,34,1]{2,1,0:T(8,128)S(1)}, f32[10,34,1]{2,1,0:T(8,128)S(1)}, u32[]{:S(2)}, u32[]{:S(2)}) collective-permute-start(f32[10,34,1]{2,1,0:T(8,128)S(1)} %get-tuple-element.64), channel_id=1, source_target_pairs={{1,0},{2,1},{3,2},{0,3},{5,4},{6,5},{7,6},{4,7},{9,8},{10,9},{11,1... | collective-permute-start | bytes 4088 | tf_op jit(solution)/shard_map/ppermute | solution.py:23
  262.0 4.4 collective-permute-start.44
  270.3 5.7 %collective-permute-start.47 = (f32[10,34,1]{2,1,0:T(8,128)S(1)}, f32[10,34,1]{2,1,0:T(8,128)S(1)}, u32[]{:S(2)}, u32[]{:S(2)}) collective-permute-start(f32[10,34,1]{2,1,0:T(8,128)S(1)} %get-tuple-element.61), channel_id=1, source_target_pairs={{0,1},{1,2},{2,3},{3,0},{4,5},{5,6},{6,7},{7,4},{8,9},{9,10},{10,1... | collective-permute-start | bytes 4088 | tf_op jit(solution)/shard_map/ppermute | solution.py:20
  272.0 5.8 %collective-permute-start.48 = (f32[10,34,1]{2,1,0:T(8,128)S(1)}, f32[10,34,1]{2,1,0:T(8,128)S(1)}, u32[]{:S(2)}, u32[]{:S(2)}) collective-permute-start(f32[10,34,1]{2,1,0:T(8,128)S(1)} %get-tuple-element.62), channel_id=1, source_target_pairs={{1,0},{2,1},{3,2},{0,3},{5,4},{6,5},{7,6},{4,7},{9,8},{10,9},{11,1... | collective-permute-start | bytes 4088 | tf_op jit(solution)/shard_map/ppermute | solution.py:23
  279.8 4.4 collective-permute-start.50
  288.3 5.7 %collective-permute-start.53 = (f32[10,34,1]{2,1,0:T(8,128)S(1)}, f32[10,34,1]{2,1,0:T(8,128)S(1)}, u32[]{:S(2)}, u32[]{:S(2)}) collective-permute-start(f32[10,34,1]{2,1,0:T(8,128)S(1)} %get-tuple-element.59), channel_id=1, source_target_pairs={{0,1},{1,2},{2,3},{3,0},{4,5},{5,6},{6,7},{7,4},{8,9},{9,10},{10,1... | collective-permute-start | bytes 4088 | tf_op jit(solution)/shard_map/ppermute | solution.py:20
  290.1 5.6 %collective-permute-start.54 = (f32[10,34,1]{2,1,0:T(8,128)S(1)}, f32[10,34,1]{2,1,0:T(8,128)S(1)}, u32[]{:S(2)}, u32[]{:S(2)}) collective-permute-start(f32[10,34,1]{2,1,0:T(8,128)S(1)} %get-tuple-element.60), channel_id=1, source_target_pairs={{1,0},{2,1},{3,2},{0,3},{5,4},{6,5},{7,6},{4,7},{9,8},{10,9},{11,1... | collective-permute-start | bytes 4088 | tf_op jit(solution)/shard_map/ppermute | solution.py:23
  297.6 4.4 collective-permute-start.56
  305.9 5.9 %collective-permute-start.59 = (f32[10,34,1]{2,1,0:T(8,128)S(1)}, f32[10,34,1]{2,1,0:T(8,128)S(1)}, u32[]{:S(2)}, u32[]{:S(2)}) collective-permute-start(f32[10,34,1]{2,1,0:T(8,128)S(1)} %get-tuple-element.57), channel_id=1, source_target_pairs={{0,1},{1,2},{2,3},{3,0},{4,5},{5,6},{6,7},{7,4},{8,9},{9,10},{10,1... | collective-permute-start | bytes 4088 | tf_op jit(solution)/shard_map/ppermute | solution.py:20
  307.2 5.7 %collective-permute-start.60 = (f32[10,34,1]{2,1,0:T(8,128)S(1)}, f32[10,34,1]{2,1,0:T(8,128)S(1)}, u32[]{:S(2)}, u32[]{:S(2)}) collective-permute-start(f32[10,34,1]{2,1,0:T(8,128)S(1)} %get-tuple-element.58), channel_id=1, source_target_pairs={{1,0},{2,1},{3,2},{0,3},{5,4},{6,5},{7,6},{4,7},{9,8},{10,9},{11,1... | collective-permute-start | bytes 4088 | tf_op jit(solution)/shard_map/ppermute | solution.py:23
  314.8 4.4 collective-permute-start.62
  323.3 5.9 %collective-permute-start.65 = (f32[10,34,1]{2,1,0:T(8,128)S(1)}, f32[10,34,1]{2,1,0:T(8,128)S(1)}, u32[]{:S(2)}, u32[]{:S(2)}) collective-permute-start(f32[10,34,1]{2,1,0:T(8,128)S(1)} %get-tuple-element.55), channel_id=1, source_target_pairs={{0,1},{1,2},{2,3},{3,0},{4,5},{5,6},{6,7},{7,4},{8,9},{9,10},{10,1... | collective-permute-start | bytes 4088 | tf_op jit(solution)/shard_map/ppermute | solution.py:20
  324.4 5.8 %collective-permute-start.66 = (f32[10,34,1]{2,1,0:T(8,128)S(1)}, f32[10,34,1]{2,1,0:T(8,128)S(1)}, u32[]{:S(2)}, u32[]{:S(2)}) collective-permute-start(f32[10,34,1]{2,1,0:T(8,128)S(1)} %get-tuple-element.56), channel_id=1, source_target_pairs={{1,0},{2,1},{3,2},{0,3},{5,4},{6,5},{7,6},{4,7},{9,8},{10,9},{11,1... | collective-permute-start | bytes 4088 | tf_op jit(solution)/shard_map/ppermute | solution.py:23
  332.1 4.4 collective-permute-start.68
  340.4 5.4 %collective-permute-start.71 = (f32[10,34,1]{2,1,0:T(8,128)S(1)}, f32[10,34,1]{2,1,0:T(8,128)S(1)}, u32[]{:S(2)}, u32[]{:S(2)}) collective-permute-start(f32[10,34,1]{2,1,0:T(8,128)S(1)} %get-tuple-element.53), channel_id=1, source_target_pairs={{0,1},{1,2},{2,3},{3,0},{4,5},{5,6},{6,7},{7,4},{8,9},{9,10},{10,1... | collective-permute-start | bytes 4088 | tf_op jit(solution)/shard_map/ppermute | solution.py:20
  341.5 5.6 %collective-permute-start.72 = (f32[10,34,1]{2,1,0:T(8,128)S(1)}, f32[10,34,1]{2,1,0:T(8,128)S(1)}, u32[]{:S(2)}, u32[]{:S(2)}) collective-permute-start(f32[10,34,1]{2,1,0:T(8,128)S(1)} %get-tuple-element.54), channel_id=1, source_target_pairs={{1,0},{2,1},{3,2},{0,3},{5,4},{6,5},{7,6},{4,7},{9,8},{10,9},{11,1... | collective-permute-start | bytes 4088 | tf_op jit(solution)/shard_map/ppermute | solution.py:23
  362.7 4.3 collective-permute-start.74
  378.9 4.3 collective-permute-start.80
  394.2 4.3 collective-permute-start.86
  409.9 4.3 collective-permute-start.92
  425.3 4.3 collective-permute-start.98
  441.4 4.8 collective-permute-start.103
  444.3 4.3 collective-permute-start.104
  448.6 9.6 %collective-permute-start.105 = (f32[6,1,64]{2,1,0:T(1,128)S(1)}, f32[6,1,64]{2,1,0:T(1,128)S(1)}, u32[]{:S(2)}, u32[]{:S(2)}) collective-permute-start(f32[6,1,64]{2,1,0:T(1,128)S(1)} %get-tuple-element.101), channel_id=1, source_target_pairs={{0,4},{4,8},{8,12},{12,0},{1,5},{5,9},{9,13},{13,1},{2,6},{6,10},{... | collective-permute-start | bytes 4616 | tf_op jit(solution)/shard_map/ppermute | solution.py:20
  448.7 9.5 %collective-permute-start.106 = (f32[6,1,64]{2,1,0:T(1,128)S(1)}, f32[6,1,64]{2,1,0:T(1,128)S(1)}, u32[]{:S(2)}, u32[]{:S(2)}) collective-permute-start(f32[6,1,64]{2,1,0:T(1,128)S(1)} %get-tuple-element.102), channel_id=1, source_target_pairs={{4,0},{8,4},{12,8},{0,12},{5,1},{9,5},{13,9},{1,13},{6,2},{10,6},{... | collective-permute-start | bytes 4616 | tf_op jit(solution)/shard_map/ppermute | solution.py:23
  458.3 4.8 collective-permute-start.107
  459.4 4.1 collective-permute-start.108
  486.3 9.7 %collective-permute-start.109 = (f32[1,32,128]{2,1,0:T(8,128)S(1)}, f32[1,32,128]{2,1,0:T(8,128)S(1)}, u32[]{:S(2)}, u32[]{:S(2)}) collective-permute-start(f32[1,32,128]{2,1,0:T(8,128)S(1)} %get-tuple-element.167), channel_id=1, source_target_pairs={{112,0},{0,16},{16,32},{32,48},{48,64},{64,80},{80,96},{96,112},{1... | collective-permute-start | bytes 49160 | tf_op jit(solution)/shard_map/ppermute | solution.py:31
  495.2 4.4 collective-permute-start.110
  499.8 4.4 collective-permute-start.112
  504.4 4.4 collective-permute-start.114
  509.0 4.4 collective-permute-start.116
  513.6 4.4 collective-permute-start.118
  518.2 4.4 collective-permute-start.120
  522.8 4.4 collective-permute-start.122
  (115 other events, 570.2 us)
where the time goes:
time: 537 us; the launch traced here: 528 us
  waiting for transfers between devices  185 us (34%)
  starting transfers between devices  138 us (26%)
  local copies, waits for them, and re-layouts  115 us (21%)
  other arithmetic  60.4 us (11%)
  blocking collectives  27.5 us (5%)
    ppermute x54, starting transfers between devices, padded_2(): lax.ppermute(lax.slice_in_dim(block, block.shape[dim] - width, None, axis...  83.7 us
    ppermute x54, waiting for transfers between devices, padded_2(): lax.ppermute(lax.slice_in_dim(block, 0, width, axis=dim), axis, backward)  81.7 us
    reshape x3, local copies, waits for them, and re-layouts, restrict(): residual.reshape(extent[0] // 2, 2, extent[1] // 2, 2, extent[2] // 2, 2)  79.2 us
    ppermute x54, waiting for transfers between devices, padded_2(): lax.ppermute(lax.slice_in_dim(block, block.shape[dim] - width, None, axis...  73.4 us
    ppermute x54, starting transfers between devices, padded_2(): lax.ppermute(lax.slice_in_dim(block, 0, width, axis=dim), axis, backward)  40.1 us
    ppermute x14, waiting for transfers between devices, passed_along(): return lax.ppermute(block, axis, route)  27.7 us
    reduce_sum x3, other arithmetic, restrict(): return 0.5 * jnp.sum(blocks, axis=(1, 3, 5))  24.9 us
    add x22, other arithmetic, smooth_with(): iterate + damping * (source_term - operator(iterate)) * inverse_diag  24.8 us
  transfers between devices with their start and end apart: 123, of which 107 were waited for; matrix products, arithmetic and copies ran while one was open for 3% of the time, Pallas kernels for 0%

commit v1 on v0

v1 whole, which is shorter than its diff:
```python
import jax
import jax.numpy as jnp
from jax import lax
from jax.experimental import pallas as pl
from jax.experimental.pallas import tpu as pltpu
from jax.sharding import PartitionSpec as P

MESH = pl.DeviceIdType.MESH
AXES = ("gx", "gy", "gz")
COUNTS = (8, 4, 4)
SWEEPS = 6
COARSE_SWEEPS = 8
HALO = 6
XO = 8
YO = 16
LANES = 128
DAMPING = 0.8

LEVELS = (
    dict(x=16, y=64, own=2, tiles=3, block=8, reach=1, shape=(3, 3, 32, 96, LANES)),
    dict(x=8, y=32, own=1, tiles=2, block=8, reach=1, shape=(3, 2, 24, 64, LANES)),
    dict(x=4, y=16, own=1, tiles=1, block=4, reach=2, shape=(3, 1, 20, 48, LANES)),
)


def coordinates():
    return tuple(lax.axis_index(a) for a in AXES)


def device_at(place, offset):
    return tuple(
        lax.rem(p + (o + n), n) if o else p for p, o, n in zip(place, offset, COUNTS)
    )


def offsets_of(level):
    reach = level["reach"]
    return [
        (dx, dy, dz)
        for dx in range(-reach, reach + 1)
        for dy in (-1, 0, 1)
        for dz in (-1, 0, 1)
        if (dx, dy, dz) != (0, 0, 0)
    ]


FACES = ((1, 0, 0), (-1, 0, 0), (0, 1, 0), (0, -1, 0), (0, 0, 1), (0, 0, -1))
PROFILE_PEERS = ((0, 0, 1), (0, 0, -1), (0, 0, 2))
COLUMN_PEERS = tuple(
    (dx, dy, 0) for dx in (4, 3, -3, 2, -2, 1, -1, 0) for dy in (2, 1, -1, 0) if (dx, dy) != (0, 0)
)


def lane_iota(rows=8):
    return lax.broadcasted_iota(jnp.int32, (rows, LANES), 1)


def select_dot(rows, picks):
    return jnp.dot(
        rows, picks, preferred_element_type=jnp.float32, precision=lax.Precision.HIGHEST
    )


def halving(shift, value, parity=None):
    k = lax.broadcasted_iota(jnp.int32, (LANES, LANES), 0)
    l = 2 * (lax.broadcasted_iota(jnp.int32, (LANES, LANES), 1) - shift)
    if parity is None:
        hit = (k == l) | (k == l + 1)
    else:
        hit = k == l + parity
    return jnp.where(hit, jnp.float32(value), jnp.float32(0.0))


def message(level, raw, packed, ext, received, offset):
    dx, dy, dz = offset
    nx, ny, own = level["x"], level["y"], level["own"]
    if dz == 0:
        if dx == 0:
            sx, tx, width = 0, XO, nx
        elif dx > 0:
            width = min(nx, HALO - (dx - 1) * nx)
            sx, tx = nx - width, XO - (dx - 1) * nx - width
        else:
            width = min(nx, HALO - (-dx - 1) * nx)
            sx, tx = 0, XO + nx + (-dx - 1) * nx
        if dy == 0:
            sy, ty, rows = 0, YO, ny
        elif dy > 0:
            sy, ty, rows = ny - 8, YO - 8, 8
        else:
            sy, ty, rows = 0, YO + ny, 8
        return (
            raw.at[pl.ds(0, own), pl.ds(sx, width), pl.ds(sy, rows), :],
            ext.at[0, pl.ds(0, own), pl.ds(tx, width), pl.ds(ty, rows), :],
        )
    blocks, strips, reach = nx // level["block"], ny // 8, level["reach"]
    if dx == 0:
        sb, tb, nb = 0, reach, blocks
    elif dx > 0:
        sb, tb, nb = blocks - 1, reach - dx, 1
    else:
        sb, tb, nb = 0, reach + blocks - 1 - dx, 1
    if dy == 0:
        ss, ts, ns = 0, 1, strips
    elif dy > 0:
        ss, ts, ns = strips - 1, 0, 1
    else:
        ss, ts, ns = 0, strips + 1, 1
    return (
        packed.at[pl.ds(sb, nb), pl.ds(ss, ns), :, :],
        received.at[0 if dz > 0 else 1, pl.ds(tb, nb), pl.ds(ts, ns), :, :],
    )


def pack_faces(level, raw, packed):
    lane = lane_iota()
    group = lane // 8
    own, block, strips = level["own"], level["block"], level["y"] // 8
    far = 15 if level["tiles"] > 1 else 7

    def strip(s, carry):
        rows = pl.ds(pl.multiple_of(8 * s, 8), 8)
        for b in range(level["x"] // block):
            total = jnp.zeros((8, LANES), jnp.float32)
            for i in range(block):
                ends = raw[0, b * block + i, rows, :]
                if own == 2:
                    ends = jnp.where(lane < 64, ends, raw[1, b * block + i, rows, :])
                moved = pltpu.roll(ends, 16 * i, 1) if i else ends
                mine = (group == 2 * i) | (group == (2 * i + far) % 16)
                total = jnp.where(mine, moved, total)
            packed[b, s] = total
        return carry

    lax.fori_loop(0, strips, strip, 0)


def stencil(level_tiles, wanted, ext, slot, x, row, coefs):
    lane = lane_iota()
    centre = [ext[slot, t, x, pl.ds(row, 8), :] for t in range(level_tiles)]
    up = [pltpu.roll(v, 1, 1) for v in centre]
    down = [pltpu.roll(v, LANES - 1, 1) for v in centre]
    sums = []
    for t in range(wanted):
        beneath, overhead = up[t], down[t]
        if level_tiles > 1:
            beneath = jnp.where(lane == 0, up[t - 1], beneath)
            overhead = jnp.where(lane == LANES - 1, down[(t + 1) % level_tiles], overhead)
        around = (
            ext[slot, t, x - 1, pl.ds(row, 8), :] + ext[slot, t, x + 1, pl.ds(row, 8), :]
        ) + (ext[slot, t, x, pl.ds(row - 1, 8), :] + ext[slot, t, x, pl.ds(row + 1, 8), :])
        c, low, high, _, _ = coefs[t]
        sums.append(c * around + (low * beneath + high * overhead))
    return centre, sums


def sweep_slots(s):
    source = jnp.where(s == 1, 0, 1 + lax.rem(s, 2))
    return source, 1 + lax.rem(s + 1, 2)


def relax(level, ext, coefs):
    tiles, nx, strips = level["tiles"], level["x"], level["y"] // 8 + 2

    def sweep(s, carry):
        source, target = sweep_slots(s)

        def plane(x, inner):
            for j in range(strips):
                row = 8 + 8 * j
                centre, sums = stencil(tiles, tiles, ext, source, x, row, coefs)
                for t in range(tiles):
                    beta = ext[0, t, x, pl.ds(row, 8), :]
                    ext[target, t, x, pl.ds(row, 8), :] = (0.2 * centre[t] + beta) + sums[t]
            return inner

        lax.fori_loop(XO - HALO + s, XO + nx + HALO - s, plane, 0)
        return carry

    lax.fori_loop(1, SWEEPS, sweep, 0)


def begin(level, raw, received, ext, coefs):
    tiles, own, nx, block = level["tiles"], level["own"], level["x"], level["block"]
    strips = level["y"] // 8 + 2
    lane = lane_iota()
    even = lax.rem(lane // 8, 2) == 0
    base = 64 if tiles == 1 else 0

    def halo_tile(x, j):
        e, i = x // block, lax.rem(x, block)
        both = jnp.where(even, received[1, e, j], received[0, e, j])
        return pltpu.roll(both, lax.rem(base + LANES - 16 * i, LANES), 1)

    def plane_of(inside):
        def plane(x, carry):
            for j in range(strips):
                row = 8 + 8 * j
                ends = halo_tile(x, j)
                for t in range(own):
                    if inside and 0 < j < strips - 1:
                        b = raw[t, x - XO, pl.ds(8 * (j - 1), 8), :]
                    else:
                        b = ext[0, t, x, pl.ds(row, 8), :]
                    if tiles == 1:
                        b = jnp.where(lane < 64, b, ends)
                    ext[0, t, x, pl.ds(row, 8), :] = b * coefs[t][3]
                if tiles > 1:
                    ext[0, own, x, pl.ds(row, 8), :] = ends * coefs[own][3]
            return carry

        return plane

    lax.fori_loop(XO - HALO, XO, plane_of(False), 0)
    lax.fori_loop(XO, XO + nx, plane_of(True), 0)
    lax.fori_loop(XO + nx, XO + nx + HALO, plane_of(False), 0)


def residual_rows(level, ext, coefs, pair, halved):
    tiles, own, nx, ny = level["tiles"], level["own"], level["x"], level["y"]
    slot = 1

    def planes(p, carry):
        for j in range(ny // 8):
            row = YO + 8 * j
            total = [None] * own
            for k in range(2):
                x = XO + 2 * p + k
                centre, sums = stencil(tiles, own, ext, slot, x, row, coefs)
                for t in range(own):
                    beta = ext[0, t, x, pl.ds(row, 8), :]
                    r = (beta - 0.8 * centre[t]) + sums[t]
                    total[t] = r if k == 0 else total[t] + r
            for t in range(own):
                pair[t, pl.ds(8 * j, 8), :] = total[t] * coefs[t][4]
        for t in range(own):
            halved[t, p] = (
                pair[t, pl.ds(0, ny // 2, stride=2), :] + pair[t, pl.ds(1, ny // 2, stride=2), :]
            )
        return carry

    lax.fori_loop(0, nx // 2, planes, 0)


def kernel(
    source_ref,
    cell_ref,
    face_ref,
    smooth_ref,
    coarse_ref,
    raw0,
    raw1,
    raw2,
    ext0,
    ext1,
    ext2,
    ext3,
    packed0,
    packed1,
    packed2,
    received0,
    received1,
    received2,
    profile,
    tables,
    spread,
    constants,
    pair,
    halved0,
    halved1,
    halved2,
    column,
    slab,
    send,
    recv,
    local,
    greet,
):
    place = coordinates()
    gx, gy, gz = place
    counter = [0]

    def remote(source, target, offset):
        k = counter[0]
        counter[0] += 1
        return pltpu.make_async_remote_copy(
            src_ref=source,
            dst_ref=target,
            send_sem=send.at[k],
            recv_sem=recv.at[k],
            device_id=device_at(place, offset),
            device_id_type=MESH,
        )

    raws, exts = (raw0, raw1, raw2), (ext0, ext1, ext2)
    packs, receiveds = (packed0, packed1, packed2), (received0, received1, received2)
    halveds = (halved0, halved1, halved2)

    barrier = pltpu.get_barrier_semaphore()
    peers = FACES + ((0, 0, 2),)
    for offset in peers:
        pl.semaphore_signal(
            barrier, inc=1, device_id=device_at(place, offset), device_id_type=MESH
        )
    loads = [
        pltpu.make_async_copy(
            source_ref.at[:, :, pl.ds(LANES * t, LANES)], raw0.at[t], local.at[t]
        )
        for t in range(2)
    ]
    for c in loads:
        c.start()
    mine = profile.at[gz]
    for t in range(2):
        profile[gz, pl.ds(t, 1), :] = cell_ref[pl.ds(LANES * t, LANES)].reshape(1, LANES)
        profile[gz, pl.ds(2 + t, 1), :] = face_ref[pl.ds(LANES * t, LANES)].reshape(1, LANES)
    for c in loads:
        c.wait()
    pack_faces(LEVELS[0], raw0, packed0)
    pl.semaphore_wait(barrier, len(peers))

    pending = []
    copies = {}
    for offset in offsets_of(LEVELS[0]):
        copies[offset] = remote(
            *message(LEVELS[0], raw0, packed0, ext0, received0, offset), offset
        )
    profiles = [remote(mine, mine, offset) for offset in PROFILE_PEERS]
    for offset in FACES:
        copies[offset].start()
    for c in profiles:
        c.start()
    for stage, distance in ((0, 2), (1, 3)):
        for offset in FACES:
            pl.semaphore_signal(
                greet.at[stage], inc=1, device_id=device_at(place, offset), device_id_type=MESH
            )
        pl.semaphore_wait(greet.at[stage], len(FACES))
        for offset in copies:
            if sum(abs(o) for o in offset) == distance:
                copies[offset].start()
    pending += list(copies.values()) + profiles

    for c in profiles:
        c.wait_recv()
    lane = lane_iota()
    row = lax.broadcasted_iota(jnp.int32, (8, LANES), 0)
    for z in range(4):
        for t in range(2):
            tables[0, pl.ds(2 * z + t, 1), :] = profile[z, pl.ds(t, 1), :]
            tables[1, pl.ds(2 * z + t, 1), :] = profile[z, pl.ds(2 + t, 1), :]
    cell, below = tables[0], tables[1]
    turned = pltpu.roll(below, LANES - 1, 1)
    above = jnp.where(lane == LANES - 1, pltpu.roll(turned, 7, 0), turned)
    above = jnp.where((row == 7) & (lane == LANES - 1), 0.0, above)
    first, second = halving(0, 1.0, 0), halving(0, 1.0, 1)
    first, second = first + halving(64, 1.0, 0), second + halving(64, 1.0, 1)
    for n in range(4):
        scale = DAMPING / (4.0 * cell + below + above)
        constants[n, 0] = cell * scale
        constants[n, 1] = jnp.where((row == 0) & (lane == 0), 0.0, below * scale)
        constants[n, 2] = above * scale
        constants[n, 3] = scale
        constants[n, 4] = (4.0 * cell + below + above) * (1.0 / DAMPING)
        if n < 3:
            spread[0, pl.ds(0, 8), :] = 0.5 * (select_dot(cell, first) + select_dot(cell, second))
            spread[1, pl.ds(0, 8), :] = select_dot(below, first)
            spread[2, pl.ds(0, 8), :] = select_dot(above, second)
            narrow = [
                jnp.where(
                    lane < 64,
                    spread[k, pl.ds(0, 8, stride=2), :],
                    spread[k, pl.ds(1, 8, stride=2), :],
                )
                for k in range(3)
            ]
            used = row < 8 >> (n + 1)
            cell, below = jnp.where(used, narrow[0], 1.0), jnp.where(used, narrow[1], 1.0)
            above = jnp.where(used, narrow[2], 1.0)

    def row_of(n, k, r):
        return jnp.broadcast_to(constants[n, k, pl.ds(r, 1), :], (8, LANES))

    def level_coefs(n):
        if n == 0:
            tiles = [lambda k, t=t: row_of(0, k, 2 * gz + t) for t in range(2)]
            tiles.append(
                lambda k: jnp.where(
                    lane < 64,
                    row_of(0, k, lax.rem(2 * gz + 2, 8)),
                    row_of(0, k, lax.rem(2 * gz + 7, 8)),
                )
            )
        elif n == 1:
            tiles = [
                lambda k: row_of(1, k, gz),
                lambda k: jnp.where(
                    lane < 64,
                    row_of(1, k, lax.rem(gz + 1, 4)),
                    row_of(1, k, lax.rem(gz + 3, 4)),
                ),
            ]
        elif n == 2:

            def one(k):
                here, there = row_of(2, k, gz // 2), row_of(2, k, 1 - gz // 2)
                lower = jnp.where(lane < 96, here, there)
                upper = pltpu.roll(jnp.where(lane < 32, there, here), 64, 1)
                return jnp.where(lax.rem(gz, 2) == 0, lower, upper)

            tiles = [one]
        else:
            tiles = [lambda k: row_of(3, k, 0)]
        return [[tile(k) for k in range(5)] for tile in tiles]

    for n, level in enumerate(LEVELS):
        raw, ext, packed, received, halved = raws[n], exts[n], packs[n], receiveds[n], halveds[n]
        if n > 0:
            pack_faces(level, raw, packed)
            copies = {}
            order = sorted(offsets_of(level), key=lambda o: -sum(abs(i) for i in o))
            for offset in order:
                copies[offset] = remote(
                    *message(level, raw, packed, ext, received, offset), offset
                )
                copies[offset].start()
            pending += list(copies.values())
        coefs = level_coefs(n)
        for c in copies.values():
            c.wait_recv()
        begin(level, raw, received, ext, coefs)
        relax(level, ext, coefs)
        if n == 0:
            stores = [
                pltpu.make_async_copy(
                    ext0.at[1, t, pl.ds(XO, 16), pl.ds(YO, 64), :],
                    smooth_ref.at[:, :, pl.ds(LANES * t, LANES)],
                    local.at[2 + t],
                )
                for t in range(2)
            ]
            for c in stores:
                c.start()
        residual_rows(level, ext, coefs, pair, halved)
        if n == 0:
            total = select_dot(halved[0].reshape(256, LANES), halving(0, 0.5)) + select_dot(
                halved[1].reshape(256, LANES), halving(64, 0.5)
            )
            raw1[0] = total.reshape(8, 32, LANES)
        elif n == 1:
            raw2[0] = select_dot(halved[0].reshape(64, LANES), halving(0, 0.5)).reshape(
                4, 16, LANES
            )
        else:
            k = lax.broadcasted_iota(jnp.int32, (LANES, LANES), 0)
            picks = jnp.where(k < 64, halving(32 * gz, 0.5), 0.0)
            column[gz] = select_dot(halved[0].reshape(16, LANES), picks).reshape(2, 8, LANES)

    copies = [remote(column.at[gz], column.at[gz], offset) for offset in PROFILE_PEERS]
    for c in copies:
        c.start()
    pending += copies
    coefs = level_coefs(3)
    for c in copies:
        c.wait_recv()
    whole = (column[0] + column[1]) + (column[2] + column[3])
    slab[...] = whole
    strip = pl.ds(pl.multiple_of(8 + 8 * gy, 8), 8)
    copies = [
        remote(slab, ext3.at[0, 0, pl.ds(8 - 2 * offset[0], 2), strip, :], offset)
        for offset in COLUMN_PEERS
    ]
    for c in copies:
        c.start()
    ext3[0, 0, pl.ds(8, 2), strip, :] = whole
    for c in pending:
        c.wait_send()
    for c in copies:
        c.wait_recv()

    def wrapped(slot, x, values):
        for j in range(6):
            ext3[slot, 0, x, pl.ds(8 * j, 8), :] = values[(j - 1) % 4]

    ext3[0, 0, 16] = ext3[0, 0, 0]

    def start_all(x, carry):
        wrapped(0, x, [ext3[0, 0, x, pl.ds(8 + 8 * j, 8), :] * coefs[0][3] for j in range(4)])
        return carry

    lax.fori_loop(1, 17, start_all, 0)

    def coarse_sweep(s, carry):
        source, target = sweep_slots(s)

        def plane(x, inner):
            values = []
            for j in range(4):
                r = 8 + 8 * j
                centre, sums = stencil(1, 1, ext3, source, x, r, coefs)
                beta = ext3[0, 0, x, pl.ds(r, 8), :]
                values.append((0.2 * centre[0] + beta) + sums[0])
            wrapped(target, x, values)
            return inner

        lax.fori_loop(1 + s, 17 - s, plane, 0)
        return carry

    lax.fori_loop(1, COARSE_SWEEPS, coarse_sweep, 0)
    coarse_ref[...] = ext3[1, 0, pl.ds(8, 2), pl.ds(8, 32), :]
    for c in copies:
        c.wait_send()
    for c in stores:
        c.wait()


def on_device(source, cell, face):
    f32 = jnp.float32
    messages = sum(len(offsets_of(level)) for level in LEVELS) + 6 + len(COLUMN_PEERS)
    vmem = pl.BlockSpec(memory_space=pltpu.VMEM)
    hbm = pl.BlockSpec(memory_space=pl.ANY)
    tile = (8, LANES)
    return pl.pallas_call(
        kernel,
        out_shape=(
            jax.ShapeDtypeStruct((16, 64, 256), f32),
            jax.ShapeDtypeStruct((2, 32, 128), f32),
        ),
        in_specs=[hbm, vmem, vmem],
        out_specs=(hbm, vmem),
        scratch_shapes=[
            pltpu.VMEM((2, 16, 64, LANES), f32),
            pltpu.VMEM((1, 8, 32, LANES), f32),
            pltpu.VMEM((1, 4, 16, LANES), f32),
            pltpu.VMEM(LEVELS[0]["shape"], f32),
            pltpu.VMEM(LEVELS[1]["shape"], f32),
            pltpu.VMEM(LEVELS[2]["shape"], f32),
            pltpu.VMEM((3, 1, 18, 48, LANES), f32),
            pltpu.VMEM((2, 8) + tile, f32),
            pltpu.VMEM((1, 4) + tile, f32),
            pltpu.VMEM((1, 2) + tile, f32),
            pltpu.VMEM((2, 4, 10) + tile, f32),
            pltpu.VMEM((2, 3, 6) + tile, f32),
            pltpu.VMEM((2, 5, 4) + tile, f32),
            pltpu.VMEM((4,) + tile, f32),
            pltpu.VMEM((2,) + tile, f32),
            pltpu.VMEM((3, 16, LANES), f32),
            pltpu.VMEM((4, 5) + tile, f32),
            pltpu.VMEM((2, 64, LANES), f32),
            pltpu.VMEM((2, 8, 32, LANES), f32),
            pltpu.VMEM((1, 4, 16, LANES), f32),
            pltpu.VMEM((1, 2, 8, LANES), f32),
            pltpu.VMEM((4, 2) + tile, f32),
            pltpu.VMEM((2,) + tile, f32),
            pltpu.SemaphoreType.DMA((messages,)),
            pltpu.SemaphoreType.DMA((messages,)),
            pltpu.SemaphoreType.DMA((4,)),
            pltpu.SemaphoreType.REGULAR((2,)),
        ],
        compiler_params=pltpu.CompilerParams(
            collective_id=0, has_side_effects=True, vmem_limit_bytes=48 << 20
        ),
    )(source, cell, face)


def solution(mesh):
    return jax.shard_map(
        on_device,
        mesh=mesh,
        in_specs=(P("gx", "gy", "gz"), P("gz"), P("gz")),
        out_specs=(P("gx", "gy", "gz"), P("gx", None, None)),
        check_vma=False,
    )
```

time: 537 us -> 195 us (0.36)
  the two profiles are of different devices: /device:TPU:57 before, /device:TPU:1 now
where the time goes in v1:
time: 195 us
  Pallas kernels  190 us (97%)
  local copies, waits for them, and re-layouts  4.16 us (2%)
    pallas_call x1, Pallas kernels, on_device(): pl.pallas_call(kernel, out_shape=(jax.ShapeDtypeStruct((16, 64, 256), f32...  190 us
    unnamed x8, local copies, waits for them, and re-layouts  4.16 us

profile of v1, /device:TPU:1, one launch (start us, length us, event | category | flops | bytes accessed | tf_op | source)
XLA Modules:
  0.0 195.1 jit_solution(3857574135026405975)
XLA Ops:
  0.6 0.0 copy-start
  0.6 1.2 copy-done
  1.9 0.0 copy-start.1
  1.9 0.7 copy-done.1
  2.5 0.0 copy-start.2
  2.5 0.7 copy-done.2
  3.2 190.3 %shard_map.50 = (f32[16,64,256]{2,1,0:T(8,128)S(1)}, f32[2,32,128]{2,1,0:T(8,128)S(1)}) custom-call(f32[16,64,256]{2,1,0:T(8,128)S(1)} %copy-done, f32[256]{0:T(256)S(1)} %copy-done.1, f32[256]{0:T(256)S(1)} %copy-done.2), custom_call_target="tpu_custom_call" | custom-call | tf_op jit(solution)/shard_map/pallas_call | solution.py:523
  193.5 1.0 copy.7
  194.5 0.6 copy.8
Async XLA Ops:
  0.6 1.2 copy-start
  1.9 0.7 copy-start.1
  2.5 0.7 copy-start.2

commit v2 on v1

--- a/solution.py
+++ b/solution.py
@@ -17,9 +17,9 @@
 DAMPING = 0.8
 
 LEVELS = (
-    dict(x=16, y=64, own=2, tiles=3, block=8, reach=1, shape=(3, 3, 32, 96, LANES)),
-    dict(x=8, y=32, own=1, tiles=2, block=8, reach=1, shape=(3, 2, 24, 64, LANES)),
-    dict(x=4, y=16, own=1, tiles=1, block=4, reach=2, shape=(3, 1, 20, 48, LANES)),
+    dict(x=16, y=64, own=2, tiles=3, block=8, reach=1, shape=(3, 32, 96, LANES)),
+    dict(x=8, y=32, own=1, tiles=2, block=8, reach=1, shape=(2, 24, 64, LANES)),
+    dict(x=4, y=16, own=1, tiles=1, block=4, reach=2, shape=(1, 20, 48, LANES)),
 )
 
 
@@ -91,7 +91,7 @@
             sy, ty, rows = 0, YO + ny, 8
         return (
             raw.at[pl.ds(0, own), pl.ds(sx, width), pl.ds(sy, rows), :],
-            ext.at[0, pl.ds(0, own), pl.ds(tx, width), pl.ds(ty, rows), :],
+            ext.at[pl.ds(0, own), pl.ds(tx, width), pl.ds(ty, rows), :],
         )
     blocks, strips, reach = nx // level["block"], ny // 8, level["reach"]
     if dx == 0:
@@ -135,9 +135,9 @@
     lax.fori_loop(0, strips, strip, 0)
 
 
-def stencil(level_tiles, wanted, ext, slot, x, row, coefs):
+def stencil(level_tiles, wanted, ext, x, row, coefs):
     lane = lane_iota()
-    centre = [ext[slot, t, x, pl.ds(row, 8), :] for t in range(level_tiles)]
+    centre = [ext[t, x, pl.ds(row, 8), :] for t in range(level_tiles)]
     up = [pltpu.roll(v, 1, 1) for v in centre]
     down = [pltpu.roll(v, LANES - 1, 1) for v in centre]
     sums = []
@@ -147,37 +147,53 @@
             beneath = jnp.where(lane == 0, up[t - 1], beneath)
             overhead = jnp.where(lane == LANES - 1, down[(t + 1) % level_tiles], overhead)
         around = (
-            ext[slot, t, x - 1, pl.ds(row, 8), :] + ext[slot, t, x + 1, pl.ds(row, 8), :]
-        ) + (ext[slot, t, x, pl.ds(row - 1, 8), :] + ext[slot, t, x, pl.ds(row + 1, 8), :])
+            ext[t, x - 1, pl.ds(row, 8), :] + ext[t, x + 1, pl.ds(row, 8), :]
+        ) + (ext[t, x, pl.ds(row - 1, 8), :] + ext[t, x, pl.ds(row + 1, 8), :])
         c, low, high, _, _ = coefs[t]
         sums.append(c * around + (low * beneath + high * overhead))
     return centre, sums
 
 
-def sweep_slots(s):
-    source = jnp.where(s == 1, 0, 1 + lax.rem(s, 2))
-    return source, 1 + lax.rem(s + 1, 2)
-
-
-def relax(level, ext, coefs):
+def update(tiles, beta, source, target, first, last, strips, coefs, finish):
+    def plane(x, carry):
+        values = []
+        for j in range(strips):
+            row = 8 + 8 * j
+            centre, sums = stencil(tiles, tiles, source, x, row, coefs)
+            for t in range(tiles):
+                if source is beta:
+                    values.append(1.2 * centre[t] + sums[t])
+                else:
+                    values.append((0.2 * centre[t] + beta[t, x, pl.ds(row, 8), :]) + sums[t])
+        finish(target, x, values)
+        return carry
+
+    lax.fori_loop(first, last, plane, 0)
+
+
+def sweeps(tiles, beta, ping, pong, first, last, count, strips, coefs, finish):
+    update(tiles, beta, beta, ping, first + 1, last - 1, strips, coefs, finish)
+
+    def two(k, carry):
+        s = 2 * k + 2
+        update(tiles, beta, ping, pong, first + s, last - s, strips, coefs, finish)
+        update(tiles, beta, pong, ping, first + s + 1, last - s - 1, strips, coefs, finish)
+        return carry
+
+    lax.fori_loop(0, (count - 1) // 2, two, 0)
+
+
+def relax(level, ext, ping, pong, coefs):
     tiles, nx, strips = level["tiles"], level["x"], level["y"] // 8 + 2
 
-    def sweep(s, carry):
-        source, target = sweep_slots(s)
-
-        def plane(x, inner):
-            for j in range(strips):
-                row = 8 + 8 * j
-                centre, sums = stencil(tiles, tiles, ext, source, x, row, coefs)
-                for t in range(tiles):
-                    beta = ext[0, t, x, pl.ds(row, 8), :]
-                    ext[target, t, x, pl.ds(row, 8), :] = (0.2 * centre[t] + beta) + sums[t]
-            return inner
-
-        lax.fori_loop(XO - HALO + s, XO + nx + HALO - s, plane, 0)
-        return carry
-
-    lax.fori_loop(1, SWEEPS, sweep, 0)
+    def finish(target, x, values):
+        for j in range(strips):
+            for t in range(tiles):
+                target[t, x, pl.ds(8 + 8 * j, 8), :] = values[j * tiles + t]
+
+    sweeps(
+        tiles, ext, ping, pong, XO - HALO, XO + nx + HALO, SWEEPS - 1, strips, coefs, finish
+    )
 
 
 def begin(level, raw, received, ext, coefs):
@@ -201,12 +217,12 @@
                     if inside and 0 < j < strips - 1:
                         b = raw[t, x - XO, pl.ds(8 * (j - 1), 8), :]
                     else:
-                        b = ext[0, t, x, pl.ds(row, 8), :]
+                        b = ext[t, x, pl.ds(row, 8), :]
                     if tiles == 1:
                         b = jnp.where(lane < 64, b, ends)
-                    ext[0, t, x, pl.ds(row, 8), :] = b * coefs[t][3]
+                    ext[t, x, pl.ds(row, 8), :] = b * coefs[t][3]
                 if tiles > 1:
-                    ext[0, own, x, pl.ds(row, 8), :] = ends * coefs[own][3]
+                    ext[own, x, pl.ds(row, 8), :] = ends * coefs[own][3]
             return carry
 
         return plane
@@ -216,9 +232,8 @@
     lax.fori_loop(XO + nx, XO + nx + HALO, plane_of(False), 0)
 
 
-def residual_rows(level, ext, coefs, pair, halved):
+def residual_rows(level, ext, ping, coefs, pair, halved):
     tiles, own, nx, ny = level["tiles"], level["own"], level["x"], level["y"]
-    slot = 1
 
     def planes(p, carry):
         for j in range(ny // 8):
@@ -226,9 +241,9 @@
             total = [None] * own
             for k in range(2):
                 x = XO + 2 * p + k
-                centre, sums = stencil(tiles, own, ext, slot, x, row, coefs)
+                centre, sums = stencil(tiles, own, ping, x, row, coefs)
                 for t in range(own):
-                    beta = ext[0, t, x, pl.ds(row, 8), :]
+                    beta = ext[t, x, pl.ds(row, 8), :]
                     r = (beta - 0.8 * centre[t]) + sums[t]
                     total[t] = r if k == 0 else total[t] + r
             for t in range(own):
@@ -255,6 +270,14 @@
     ext1,
     ext2,
     ext3,
+    ping0,
+    ping1,
+    ping2,
+    ping3,
+    pong0,
+    pong1,
+    pong2,
+    pong3,
     packed0,
     packed1,
     packed2,
@@ -292,6 +315,7 @@
             device_id_type=MESH,
         )
 
+    pings, pongs = (ping0, ping1, ping2), (pong0, pong1, pong2)
     raws, exts = (raw0, raw1, raw2), (ext0, ext1, ext2)
     packs, receiveds = (packed0, packed1, packed2), (received0, received1, received2)
     halveds = (halved0, halved1, halved2)
@@ -429,11 +453,11 @@
         for c in copies.values():
             c.wait_recv()
         begin(level, raw, received, ext, coefs)
-        relax(level, ext, coefs)
+        relax(level, ext, pings[n], pongs[n], coefs)
         if n == 0:
             stores = [
                 pltpu.make_async_copy(
-                    ext0.at[1, t, pl.ds(XO, 16), pl.ds(YO, 64), :],
+                    ping0.at[t, pl.ds(XO, 16), pl.ds(YO, 64), :],
                     smooth_ref.at[:, :, pl.ds(LANES * t, LANES)],
                     local.at[2 + t],
                 )
@@ -441,7 +465,7 @@
             ]
             for c in stores:
                 c.start()
-        residual_rows(level, ext, coefs, pair, halved)
+        residual_rows(level, ext, pings[n], coefs, pair, halved)
         if n == 0:
             total = select_dot(halved[0].reshape(256, LANES), halving(0, 0.5)) + select_dot(
                 halved[1].reshape(256, LANES), halving(64, 0.5)
@@ -467,47 +491,31 @@
     slab[...] = whole
     strip = pl.ds(pl.multiple_of(8 + 8 * gy, 8), 8)
     copies = [
-        remote(slab, ext3.at[0, 0, pl.ds(8 - 2 * offset[0], 2), strip, :], offset)
+        remote(slab, ext3.at[0, pl.ds(8 - 2 * offset[0], 2), strip, :], offset)
         for offset in COLUMN_PEERS
     ]
     for c in copies:
         c.start()
-    ext3[0, 0, pl.ds(8, 2), strip, :] = whole
+    ext3[0, pl.ds(8, 2), strip, :] = whole
     for c in pending:
         c.wait_send()
     for c in copies:
         c.wait_recv()
 
-    def wrapped(slot, x, values):
+    def wrapped(target, x, values):
         for j in range(6):
-            ext3[slot, 0, x, pl.ds(8 * j, 8), :] = values[(j - 1) % 4]
-
-    ext3[0, 0, 16] = ext3[0, 0, 0]
+            target[0, x, pl.ds(8 * j, 8), :] = values[(j - 1) % 4]
+
+    ext3[0, 16] = ext3[0, 0]
 
     def start_all(x, carry):
-        wrapped(0, x, [ext3[0, 0, x, pl.ds(8 + 8 * j, 8), :] * coefs[0][3] for j in range(4)])
+        wrapped(ext3, x, [ext3[0, x, pl.ds(8 + 8 * j, 8), :] * coefs[0][3] for j in range(4)])
         return carry
 
     lax.fori_loop(1, 17, start_all, 0)
 
-    def coarse_sweep(s, carry):
-        source, target = sweep_slots(s)
-
-        def plane(x, inner):
-            values = []
-            for j in range(4):
-                r = 8 + 8 * j
-                centre, sums = stencil(1, 1, ext3, source, x, r, coefs)
-                beta = ext3[0, 0, x, pl.ds(r, 8), :]
-                values.append((0.2 * centre[0] + beta) + sums[0])
-            wrapped(target, x, values)
-            return inner
-
-        lax.fori_loop(1 + s, 17 - s, plane, 0)
-        return carry
-
-    lax.fori_loop(1, COARSE_SWEEPS, coarse_sweep, 0)
-    coarse_ref[...] = ext3[1, 0, pl.ds(8, 2), pl.ds(8, 32), :]
+    sweeps(1, ext3, ping3, pong3, 1, 17, COARSE_SWEEPS - 1, 4, coefs, wrapped)
+    coarse_ref[...] = ping3[0, pl.ds(8, 2), pl.ds(8, 32), :]
     for c in copies:
         c.wait_send()
     for c in stores:
@@ -535,7 +543,15 @@
             pltpu.VMEM(LEVELS[0]["shape"], f32),
             pltpu.VMEM(LEVELS[1]["shape"], f32),
             pltpu.VMEM(LEVELS[2]["shape"], f32),
-            pltpu.VMEM((3, 1, 18, 48, LANES), f32),
+            pltpu.VMEM((1, 18, 48, LANES), f32),
+            pltpu.VMEM(LEVELS[0]["shape"], f32),
+            pltpu.VMEM(LEVELS[1]["shape"], f32),
+            pltpu.VMEM(LEVELS[2]["shape"], f32),
+            pltpu.VMEM((1, 18, 48, LANES), f32),
+            pltpu.VMEM(LEVELS[0]["shape"], f32),
+            pltpu.VMEM(LEVELS[1]["shape"], f32),
+            pltpu.VMEM(LEVELS[2]["shape"], f32),
+            pltpu.VMEM((1, 18, 48, LANES), f32),
             pltpu.VMEM((2, 8) + tile, f32),
             pltpu.VMEM((1, 4) + tile, f32),
             pltpu.VMEM((1, 2) + tile, f32),

time: 195 us -> 82.6 us (0.42)
  Pallas kernels: 190 us -> 77.6 us
    pallas_call x1, Pallas kernels: 190 us -> 77.6 us  [on_device(): pl.pallas_call(kernel, out_shape=(jax.ShapeDtypeStruct((16, 64, 256), f32...]
where the time goes in v2:
time: 82.6 us; the launch traced here: 82.4 us
  Pallas kernels  77.6 us (94%)
  local copies, waits for them, and re-layouts  4.16 us (5%)
    pallas_call x1, Pallas kernels, on_device(): pl.pallas_call(kernel, out_shape=(jax.ShapeDtypeStruct((16, 64, 256), f32...  77.6 us
    unnamed x8, local copies, waits for them, and re-layouts  4.16 us

profile of v2, /device:TPU:1, one launch (start us, length us, event | category | flops | bytes accessed | tf_op | source)
XLA Modules:
  0.0 82.4 jit_solution(4790990014650427195)
XLA Ops:
  0.6 0.0 copy-start
  0.6 1.2 %copy-done = f32[16,64,256]{2,1,0:T(8,128)S(1)} copy-done((f32[16,64,256]{2,1,0:T(8,128)S(1)}, f32[16,64,256]{2,1,0:T(8,128)}, u32[]{:S(2)}) %copy-start) | copy-done | bytes 1048600
  1.9 0.0 copy-start.1
  1.9 0.7 copy-done.1
  2.5 0.0 copy-start.2
  2.5 0.7 copy-done.2
  3.2 77.6 %shard_map.50 = (f32[16,64,256]{2,1,0:T(8,128)S(1)}, f32[2,32,128]{2,1,0:T(8,128)S(1)}) custom-call(f32[16,64,256]{2,1,0:T(8,128)S(1)} %copy-done, f32[256]{0:T(256)S(1)} %copy-done.1, f32[256]{0:T(256)S(1)} %copy-done.2), custom_call_target="tpu_custom_call" | custom-call | tf_op jit(solution)/shard_map/pallas_call | solution.py:531
  80.8 1.0 %copy.7 = f32[16,64,256]{2,1,0:T(8,128)} copy(f32[16,64,256]{2,1,0:T(8,128)S(1)} %get-tuple-element.4) | data formatting | bytes 2097152
  81.8 0.6 copy.8
Async XLA Ops:
  0.6 1.2 %copy-start = (f32[16,64,256]{2,1,0:T(8,128)S(1)}, f32[16,64,256]{2,1,0:T(8,128)}, u32[]{:S(2)}) copy-start(f32[16,64,256]{2,1,0:T(8,128)} %source_ref.1) | copy-start | bytes 3145732
  1.9 0.7 copy-start.1
  2.5 0.7 copy-start.2

commit v3 on v2

--- a/solution.py
+++ b/solution.py
@@ -17,9 +17,9 @@
 DAMPING = 0.8
 
 LEVELS = (
-    dict(x=16, y=64, own=2, tiles=3, block=8, reach=1, shape=(3, 32, 96, LANES)),
-    dict(x=8, y=32, own=1, tiles=2, block=8, reach=1, shape=(2, 24, 64, LANES)),
-    dict(x=4, y=16, own=1, tiles=1, block=4, reach=2, shape=(1, 20, 48, LANES)),
+    dict(x=16, y=64, own=2, tiles=3, block=8, reach=1, step=1, shape=(3, 32, 96, LANES)),
+    dict(x=8, y=32, own=1, tiles=2, block=8, reach=1, step=2, shape=(2, 24, 64, LANES)),
+    dict(x=4, y=16, own=1, tiles=1, block=4, reach=2, step=0, shape=(1, 20, 48, LANES)),
 )
 
 
@@ -154,30 +154,54 @@
     return centre, sums
 
 
-def update(tiles, beta, source, target, first, last, strips, coefs, finish):
-    def plane(x, carry):
-        values = []
-        for j in range(strips):
-            row = 8 + 8 * j
-            centre, sums = stencil(tiles, tiles, source, x, row, coefs)
-            for t in range(tiles):
-                if source is beta:
-                    values.append(1.2 * centre[t] + sums[t])
-                else:
-                    values.append((0.2 * centre[t] + beta[t, x, pl.ds(row, 8), :]) + sums[t])
-        finish(target, x, values)
+def update(tiles, beta, source, target, first, last, step, strips, coefs, finish):
+    def planes(start):
+        done = []
+        for k in range(step):
+            x = start + k
+            values = []
+            for j in range(strips):
+                row = 8 + 8 * j
+                centre, sums = stencil(tiles, tiles, source, x, row, coefs)
+                for t in range(tiles):
+                    if source is beta:
+                        values.append(1.2 * centre[t] + sums[t])
+                    else:
+                        values.append((0.2 * centre[t] + beta[t, x, pl.ds(row, 8), :]) + sums[t])
+            done.append((x, values))
+        for x, values in done:
+            finish(target, x, values)
+
+    for_each(first, last, step, planes)
+
+
+def for_each(first, last, step, body):
+    if isinstance(first, int) and last - first == step:
+        body(first)
+        return
+
+    def turn(i, carry):
+        body(first + step * i)
         return carry
 
-    lax.fori_loop(first, last, plane, 0)
-
-
-def sweeps(tiles, beta, ping, pong, first, last, count, strips, coefs, finish):
-    update(tiles, beta, beta, ping, first + 1, last - 1, strips, coefs, finish)
+    lax.fori_loop(0, (last - first) // step, turn, 0)
+
+
+def sweeps(tiles, beta, ping, pong, first, last, count, step, strips, coefs, finish):
+    if step == 0:
+        source = beta
+        for s in range(1, count + 1):
+            target = ping if s % 2 else pong
+            lo, hi = first + s, last - s
+            update(tiles, beta, source, target, lo, hi, hi - lo, strips, coefs, finish)
+            source = target
+        return
+    update(tiles, beta, beta, ping, first + 1, last - 1, step, strips, coefs, finish)
 
     def two(k, carry):
         s = 2 * k + 2
-        update(tiles, beta, ping, pong, first + s, last - s, strips, coefs, finish)
-        update(tiles, beta, pong, ping, first + s + 1, last - s - 1, strips, coefs, finish)
+        update(tiles, beta, ping, pong, first + s, last - s, step, strips, coefs, finish)
+        update(tiles, beta, pong, ping, first + s + 1, last - s - 1, step, strips, coefs, finish)
         return carry
 
     lax.fori_loop(0, (count - 1) // 2, two, 0)
@@ -192,13 +216,23 @@
                 target[t, x, pl.ds(8 + 8 * j, 8), :] = values[j * tiles + t]
 
     sweeps(
-        tiles, ext, ping, pong, XO - HALO, XO + nx + HALO, SWEEPS - 1, strips, coefs, finish
+        tiles,
+        ext,
+        ping,
+        pong,
+        XO - HALO,
+        XO + nx + HALO,
+        SWEEPS - 1,
+        level["step"],
+        strips,
+        coefs,
+        finish,
     )
 
 
 def begin(level, raw, received, ext, coefs):
     tiles, own, nx, block = level["tiles"], level["own"], level["x"], level["block"]
-    strips = level["y"] // 8 + 2
+    strips, step = level["y"] // 8 + 2, max(level["step"], 2)
     lane = lane_iota()
     even = lax.rem(lane // 8, 2) == 0
     base = 64 if tiles == 1 else 0
@@ -209,7 +243,7 @@
         return pltpu.roll(both, lax.rem(base + LANES - 16 * i, LANES), 1)
 
     def plane_of(inside):
-        def plane(x, carry):
+        def plane(x):
             for j in range(strips):
                 row = 8 + 8 * j
                 ends = halo_tile(x, j)
@@ -223,13 +257,16 @@
                     ext[t, x, pl.ds(row, 8), :] = b * coefs[t][3]
                 if tiles > 1:
                     ext[own, x, pl.ds(row, 8), :] = ends * coefs[own][3]
-            return carry
-
-        return plane
-
-    lax.fori_loop(XO - HALO, XO, plane_of(False), 0)
-    lax.fori_loop(XO, XO + nx, plane_of(True), 0)
-    lax.fori_loop(XO + nx, XO + nx + HALO, plane_of(False), 0)
+
+        def some(x):
+            for k in range(step):
+                plane(x + k)
+
+        return some
+
+    for_each(XO - HALO, XO, step, plane_of(False))
+    for_each(XO, XO + nx, step, plane_of(True))
+    for_each(XO + nx, XO + nx + HALO, step, plane_of(False))
 
 
 def residual_rows(level, ext, ping, coefs, pair, halved):
@@ -284,6 +321,7 @@
     received0,
     received1,
     received2,
+    line,
     profile,
     tables,
     spread,
@@ -332,14 +370,16 @@
         )
         for t in range(2)
     ]
+    loads.append(pltpu.make_async_copy(cell_ref, line.at[0], local.at[4]))
+    loads.append(pltpu.make_async_copy(face_ref, line.at[1], local.at[5]))
     for c in loads:
         c.start()
     mine = profile.at[gz]
-    for t in range(2):
-        profile[gz, pl.ds(t, 1), :] = cell_ref[pl.ds(LANES * t, LANES)].reshape(1, LANES)
-        profile[gz, pl.ds(2 + t, 1), :] = face_ref[pl.ds(LANES * t, LANES)].reshape(1, LANES)
     for c in loads:
         c.wait()
+    for t in range(2):
+        profile[gz, pl.ds(t, 1), :] = line[0, pl.ds(LANES * t, LANES)].reshape(1, LANES)
+        profile[gz, pl.ds(2 + t, 1), :] = line[1, pl.ds(LANES * t, LANES)].reshape(1, LANES)
     pack_faces(LEVELS[0], raw0, packed0)
     pl.semaphore_wait(barrier, len(peers))
 
@@ -514,7 +554,7 @@
 
     lax.fori_loop(1, 17, start_all, 0)
 
-    sweeps(1, ext3, ping3, pong3, 1, 17, COARSE_SWEEPS - 1, 4, coefs, wrapped)
+    sweeps(1, ext3, ping3, pong3, 1, 17, COARSE_SWEEPS - 1, 0, 4, coefs, wrapped)
     coarse_ref[...] = ping3[0, pl.ds(8, 2), pl.ds(8, 32), :]
     for c in copies:
         c.wait_send()
@@ -526,7 +566,7 @@
     f32 = jnp.float32
     messages = sum(len(offsets_of(level)) for level in LEVELS) + 6 + len(COLUMN_PEERS)
     vmem = pl.BlockSpec(memory_space=pltpu.VMEM)
-    hbm = pl.BlockSpec(memory_space=pl.ANY)
+    hbm = pl.BlockSpec(memory_space=pltpu.HBM)
     tile = (8, LANES)
     return pl.pallas_call(
         kernel,
@@ -534,7 +574,7 @@
             jax.ShapeDtypeStruct((16, 64, 256), f32),
             jax.ShapeDtypeStruct((2, 32, 128), f32),
         ),
-        in_specs=[hbm, vmem, vmem],
+        in_specs=[hbm, hbm, hbm],
         out_specs=(hbm, vmem),
         scratch_shapes=[
             pltpu.VMEM((2, 16, 64, LANES), f32),
@@ -558,6 +598,7 @@
             pltpu.VMEM((2, 4, 10) + tile, f32),
             pltpu.VMEM((2, 3, 6) + tile, f32),
             pltpu.VMEM((2, 5, 4) + tile, f32),
+            pltpu.VMEM((2, 256), f32),
             pltpu.VMEM((4,) + tile, f32),
             pltpu.VMEM((2,) + tile, f32),
             pltpu.VMEM((3, 16, LANES), f32),
@@ -570,11 +611,11 @@
             pltpu.VMEM((2,) + tile, f32),
             pltpu.SemaphoreType.DMA((messages,)),
             pltpu.SemaphoreType.DMA((messages,)),
-            pltpu.SemaphoreType.DMA((4,)),
+            pltpu.SemaphoreType.DMA((6,)),
             pltpu.SemaphoreType.REGULAR((2,)),
         ],
         compiler_params=pltpu.CompilerParams(
-            collective_id=0, has_side_effects=True, vmem_limit_bytes=48 << 20
+            collective_id=0, has_side_effects=True, vmem_limit_bytes=62 << 20
         ),
     )(source, cell, face)
 

time: 82.6 us -> 69.6 us (0.84)
  Pallas kernels: 77.6 us -> 65.9 us
  local copies, waits for them, and re-layouts: 4.16 us -> 2.92 us
    pallas_call x1, Pallas kernels: 77.6 us -> 65.9 us  [on_device(): pl.pallas_call(kernel, out_shape=(jax.ShapeDtypeStruct((16, 64, 256), f32...]
    unnamed x8 -> x4, local copies, waits for them, and re-layouts: 4.16 us -> 2.92 us
where the time goes in v3:
time: 69.6 us; the launch traced here: 69.5 us
  Pallas kernels  65.9 us (95%)
  local copies, waits for them, and re-layouts  2.92 us (4%)
    pallas_call x1, Pallas kernels, on_device(): pl.pallas_call(kernel, out_shape=(jax.ShapeDtypeStruct((16, 64, 256), f32...  65.9 us
    unnamed x4, local copies, waits for them, and re-layouts  2.92 us

profile of v3, /device:TPU:1, one launch (start us, length us, event | category | flops | bytes accessed | tf_op | source)
XLA Modules:
  0.0 69.5 jit_solution(10406142248442802674)
XLA Ops:
  0.6 65.9 %shard_map.50 = (f32[16,64,256]{2,1,0:T(8,128)}, f32[2,32,128]{2,1,0:T(8,128)}) custom-call(f32[16,64,256]{2,1,0:T(8,128)} %source_ref.1, f32[256]{0:T(256)} %cell_ref.1, f32[256]{0:T(256)} %face_ref.1), custom_call_target="tpu_custom_call" | custom-call | tf_op jit(solution)/shard_map/pallas_call | solution.py:571
  66.6 0.0 copy-start
  66.6 2.3 %copy.7 = f32[16,64,256]{2,1,0:T(8,128)} copy(f32[16,64,256]{2,1,0:T(8,128)} %get-tuple-element.4) | data formatting | bytes 2097152
  68.9 0.0 copy-done
  68.9 0.6 copy.8
Async XLA Ops:
  66.6 2.3 %copy-start = (f32[2,32,128]{2,1,0:T(8,128)S(1)}, f32[2,32,128]{2,1,0:T(8,128)}, u32[]{:S(2)}) copy-start(f32[2,32,128]{2,1,0:T(8,128)} %get-tuple-element.5) | copy-start | bytes 98308

commit v4 on v3

--- a/solution.py
+++ b/solution.py
@@ -17,9 +17,9 @@
 DAMPING = 0.8
 
 LEVELS = (
-    dict(x=16, y=64, own=2, tiles=3, block=8, reach=1, step=1, shape=(3, 32, 96, LANES)),
-    dict(x=8, y=32, own=1, tiles=2, block=8, reach=1, step=2, shape=(2, 24, 64, LANES)),
-    dict(x=4, y=16, own=1, tiles=1, block=4, reach=2, step=0, shape=(1, 20, 48, LANES)),
+    dict(x=16, y=64, own=2, split=True, tiles=3, block=8, reach=1, step=1, shape=(3, 32, 96, LANES)),
+    dict(x=8, y=32, own=1, split=False, tiles=2, block=8, reach=1, step=2, shape=(2, 24, 64, LANES)),
+    dict(x=4, y=16, own=1, split=False, tiles=1, block=4, reach=2, step=0, shape=(1, 20, 48, LANES)),
 )
 
 
@@ -59,6 +59,22 @@
     return jnp.dot(
         rows, picks, preferred_element_type=jnp.float32, precision=lax.Precision.HIGHEST
     )
+
+
+def as_bf16(hit):
+    return jnp.where(hit, jnp.float32(1.0), jnp.float32(0.0)).astype(jnp.bfloat16)
+
+
+def permuted(first, second, picks):
+    rows = first.size // LANES
+    left = jnp.concatenate([first.reshape(rows, LANES), second.reshape(rows, LANES)], axis=1)
+    total = None
+    for _ in range(3):
+        term = left.astype(jnp.bfloat16)
+        left = left - term.astype(jnp.float32)
+        part = jnp.dot(term, picks, preferred_element_type=jnp.float32)
+        total = part if total is None else total + part
+    return total
 
 
 def halving(shift, value, parity=None):
@@ -135,17 +151,42 @@
     lax.fori_loop(0, strips, strip, 0)
 
 
+def vertical(level_tiles, wanted, centre):
+    lane = lane_iota()
+
+    def up(v):
+        return pltpu.roll(v, 1, 1)
+
+    def down(v):
+        return pltpu.roll(v, LANES - 1, 1)
+
+    if level_tiles == 1:
+        return [(up(centre[0]), down(centre[0]))]
+    if level_tiles == 2:
+        ups, downs = [up(v) for v in centre], [down(v) for v in centre]
+        return [
+            (
+                jnp.where(lane == 0, ups[1 - t], ups[t]),
+                jnp.where(lane == LANES - 1, downs[1 - t], downs[t]),
+            )
+            for t in range(wanted)
+        ]
+    even, odd, halo = centre
+    up_odd, down_even, up_halo, down_halo = up(odd), down(even), up(halo), down(halo)
+    return [
+        (jnp.where(lane == 0, up_halo, up_odd), odd),
+        (even, jnp.where(lane == LANES - 1, down_halo, down_even)),
+        (
+            jnp.where(lane == 0, up_odd, up_halo),
+            jnp.where(lane == LANES - 1, down_even, down_halo),
+        ),
+    ][:wanted]
+
+
 def stencil(level_tiles, wanted, ext, x, row, coefs):
-    lane = lane_iota()
     centre = [ext[t, x, pl.ds(row, 8), :] for t in range(level_tiles)]
-    up = [pltpu.roll(v, 1, 1) for v in centre]
-    down = [pltpu.roll(v, LANES - 1, 1) for v in centre]
     sums = []
-    for t in range(wanted):
-        beneath, overhead = up[t], down[t]
-        if level_tiles > 1:
-            beneath = jnp.where(lane == 0, up[t - 1], beneath)
-            overhead = jnp.where(lane == LANES - 1, down[(t + 1) % level_tiles], overhead)
+    for t, (beneath, overhead) in enumerate(vertical(level_tiles, wanted, centre)):
         around = (
             ext[t, x - 1, pl.ds(row, 8), :] + ext[t, x + 1, pl.ds(row, 8), :]
         ) + (ext[t, x, pl.ds(row - 1, 8), :] + ext[t, x, pl.ds(row + 1, 8), :])
@@ -207,30 +248,52 @@
     lax.fori_loop(0, (count - 1) // 2, two, 0)
 
 
-def relax(level, ext, ping, pong, coefs):
-    tiles, nx, strips = level["tiles"], level["x"], level["y"] // 8 + 2
+def finisher(level):
+    tiles, strips = level["tiles"], level["y"] // 8 + 2
 
     def finish(target, x, values):
         for j in range(strips):
             for t in range(tiles):
                 target[t, x, pl.ds(8 + 8 * j, 8), :] = values[j * tiles + t]
 
+    return finish
+
+
+def relax(level, ext, ping, pong, coefs, reach):
     sweeps(
-        tiles,
+        level["tiles"],
         ext,
         ping,
         pong,
-        XO - HALO,
-        XO + nx + HALO,
+        XO - reach,
+        XO + level["x"] + reach,
         SWEEPS - 1,
         level["step"],
-        strips,
+        level["y"] // 8 + 2,
         coefs,
-        finish,
+        finisher(level),
     )
 
 
-def begin(level, raw, received, ext, coefs):
+def relax_wings(level, ext, ping, pong, coefs):
+    tiles, nx, strips = level["tiles"], level["x"], level["y"] // 8 + 2
+    finish = finisher(level)
+
+    def both(s, source, target):
+        for first in (XO - HALO + s, XO + nx - s):
+            update(tiles, ext, source, target, first, first + HALO, 1, strips, coefs, finish)
+
+    both(1, ext, ping)
+
+    def two(k, carry):
+        both(2 * k + 2, ping, pong)
+        both(2 * k + 3, pong, ping)
+        return carry
+
+    lax.fori_loop(0, (SWEEPS - 2) // 2, two, 0)
+
+
+def begin(level, raw, received, ext, coefs, parts):
     tiles, own, nx, block = level["tiles"], level["own"], level["x"], level["block"]
     strips, step = level["y"] // 8 + 2, max(level["step"], 2)
     lane = lane_iota()
@@ -264,9 +327,11 @@
 
         return some
 
-    for_each(XO - HALO, XO, step, plane_of(False))
-    for_each(XO, XO + nx, step, plane_of(True))
-    for_each(XO + nx, XO + nx + HALO, step, plane_of(False))
+    if "own" in parts:
+        for_each(XO, XO + nx, step, plane_of(True))
+    if "halo" in parts:
+        for_each(XO - HALO, XO, step, plane_of(False))
+        for_each(XO + nx, XO + nx + HALO, step, plane_of(False))
 
 
 def residual_rows(level, ext, ping, coefs, pair, halved):
@@ -283,12 +348,13 @@
                     beta = ext[t, x, pl.ds(row, 8), :]
                     r = (beta - 0.8 * centre[t]) + sums[t]
                     total[t] = r if k == 0 else total[t] + r
-            for t in range(own):
-                pair[t, pl.ds(8 * j, 8), :] = total[t] * coefs[t][4]
-        for t in range(own):
-            halved[t, p] = (
-                pair[t, pl.ds(0, ny // 2, stride=2), :] + pair[t, pl.ds(1, ny // 2, stride=2), :]
-            )
+            row_sum = total[0] * coefs[0][4]
+            if own == 2:
+                row_sum = row_sum + total[1] * coefs[1][4]
+            pair[pl.ds(8 * j, 8), :] = row_sum
+        halved[0, p] = 0.5 * (
+            pair[pl.ds(0, ny // 2, stride=2), :] + pair[pl.ds(1, ny // 2, stride=2), :]
+        )
         return carry
 
     lax.fori_loop(0, nx // 2, planes, 0)
@@ -307,6 +373,10 @@
     ext1,
     ext2,
     ext3,
+    natural,
+    sm,
+    order,
+    back,
     ping0,
     ping1,
     ping2,
@@ -326,8 +396,8 @@
     tables,
     spread,
     constants,
+    sides,
     pair,
-    halved0,
     halved1,
     halved2,
     column,
@@ -356,7 +426,7 @@
     pings, pongs = (ping0, ping1, ping2), (pong0, pong1, pong2)
     raws, exts = (raw0, raw1, raw2), (ext0, ext1, ext2)
     packs, receiveds = (packed0, packed1, packed2), (received0, received1, received2)
-    halveds = (halved0, halved1, halved2)
+    halveds = (raw1, halved1, halved2)
 
     barrier = pltpu.get_barrier_semaphore()
     peers = FACES + ((0, 0, 2),)
@@ -366,7 +436,7 @@
         )
     loads = [
         pltpu.make_async_copy(
-            source_ref.at[:, :, pl.ds(LANES * t, LANES)], raw0.at[t], local.at[t]
+            source_ref.at[:, :, pl.ds(LANES * t, LANES)], natural.at[t], local.at[t]
         )
         for t in range(2)
     ]
@@ -380,7 +450,20 @@
     for t in range(2):
         profile[gz, pl.ds(t, 1), :] = line[0, pl.ds(LANES * t, LANES)].reshape(1, LANES)
         profile[gz, pl.ds(2 + t, 1), :] = line[1, pl.ds(LANES * t, LANES)].reshape(1, LANES)
-    pack_faces(LEVELS[0], raw0, packed0)
+    z_from = lax.broadcasted_iota(jnp.int32, (256, 256), 0)
+    z_to = lax.broadcasted_iota(jnp.int32, (256, 256), 1)
+    order[...] = as_bf16(z_from == 2 * lax.rem(z_to, LANES) + z_to // LANES)
+    back[...] = as_bf16(z_to == 2 * lax.rem(z_from, LANES) + z_from // LANES)
+
+    def sort_cells(g, carry):
+        at = pl.ds(4 * g, 4)
+        moved = permuted(natural[0, at], natural[1, at], order[...])
+        raw0[0, at] = moved[:, :LANES].reshape(4, 64, LANES)
+        raw0[1, at] = moved[:, LANES:].reshape(4, 64, LANES)
+        return carry
+
+    lax.fori_loop(0, 4, sort_cells, 0)
+    pack_faces(LEVELS[0], natural, packed0)
     pl.semaphore_wait(barrier, len(peers))
 
     pending = []
@@ -390,18 +473,20 @@
             *message(LEVELS[0], raw0, packed0, ext0, received0, offset), offset
         )
     profiles = [remote(mine, mine, offset) for offset in PROFILE_PEERS]
-    for offset in FACES:
-        copies[offset].start()
     for c in profiles:
         c.start()
+    for offset in FACES[:1:-1]:
+        copies[offset].start()
     for stage, distance in ((0, 2), (1, 3)):
         for offset in FACES:
             pl.semaphore_signal(
                 greet.at[stage], inc=1, device_id=device_at(place, offset), device_id_type=MESH
             )
         pl.semaphore_wait(greet.at[stage], len(FACES))
-        for offset in copies:
+        for offset in sorted(copies, key=lambda o: abs(o[0])):
             if sum(abs(o) for o in offset) == distance:
+                copies[offset].start()
+            elif distance == 2 and offset in FACES[:2]:
                 copies[offset].start()
     pending += list(copies.values()) + profiles
 
@@ -419,35 +504,63 @@
     above = jnp.where((row == 7) & (lane == LANES - 1), 0.0, above)
     first, second = halving(0, 1.0, 0), halving(0, 1.0, 1)
     first, second = first + halving(64, 1.0, 0), second + halving(64, 1.0, 1)
-    for n in range(4):
-        scale = DAMPING / (4.0 * cell + below + above)
-        constants[n, 0] = cell * scale
-        constants[n, 1] = jnp.where((row == 0) & (lane == 0), 0.0, below * scale)
-        constants[n, 2] = above * scale
-        constants[n, 3] = scale
-        constants[n, 4] = (4.0 * cell + below + above) * (1.0 / DAMPING)
-        if n < 3:
-            spread[0, pl.ds(0, 8), :] = 0.5 * (select_dot(cell, first) + select_dot(cell, second))
-            spread[1, pl.ds(0, 8), :] = select_dot(below, first)
-            spread[2, pl.ds(0, 8), :] = select_dot(above, second)
-            narrow = [
-                jnp.where(
-                    lane < 64,
-                    spread[k, pl.ds(0, 8, stride=2), :],
-                    spread[k, pl.ds(1, 8, stride=2), :],
-                )
-                for k in range(3)
-            ]
-            used = row < 8 >> (n + 1)
-            cell, below = jnp.where(used, narrow[0], 1.0), jnp.where(used, narrow[1], 1.0)
-            above = jnp.where(used, narrow[2], 1.0)
+    picks = jnp.concatenate([first, second], axis=1)
+
+    def keep(ref, cell, below, above, bottom):
+        diag = 4.0 * cell + below + above
+        scale = DAMPING / diag
+        ref[0] = cell * scale
+        ref[1] = jnp.where((row == 0) & (lane == 0), 0.0, below * scale) if bottom else below * scale
+        ref[2] = above * scale
+        ref[3] = scale
+        ref[4] = diag * (1.0 / DAMPING)
+
+    def narrowed(n, fields):
+        halves = []
+        for k, values in enumerate(fields):
+            taken = select_dot(values, picks)
+            for p in range(2):
+                spread[k, p, pl.ds(0, 8), :] = taken[:, LANES * p : LANES * (p + 1)]
+        for k in range(3):
+            halves.append(
+                [
+                    jnp.where(
+                        row < 8 >> (n + 1),
+                        jnp.where(
+                            lane < 64,
+                            spread[k, p, pl.ds(0, 8, stride=2), :],
+                            spread[k, p, pl.ds(1, 8, stride=2), :],
+                        ),
+                        1.0,
+                    )
+                    for p in range(2)
+                ]
+            )
+        return halves
+
+    keep(constants.at[0], cell, below, above, True)
+    finest = narrowed(0, (cell, below, above))
+    for p in range(2):
+        keep(sides.at[p], *[field[p] for field in finest], p == 0)
+
+    def coarser_constants():
+        halves = finest
+        for n in range(1, 4):
+            cells, belows, aboves = halves
+            fields = (0.5 * (cells[0] + cells[1]), belows[0], aboves[1])
+            keep(constants.at[n], *fields, True)
+            if n < 3:
+                halves = narrowed(n, fields)
 
     def row_of(n, k, r):
         return jnp.broadcast_to(constants[n, k, pl.ds(r, 1), :], (8, LANES))
 
     def level_coefs(n):
         if n == 0:
-            tiles = [lambda k, t=t: row_of(0, k, 2 * gz + t) for t in range(2)]
+            tiles = [
+                lambda k, t=t: jnp.broadcast_to(sides[t, k, pl.ds(gz, 1), :], (8, LANES))
+                for t in range(2)
+            ]
             tiles.append(
                 lambda k: jnp.where(
                     lane < 64,
@@ -477,6 +590,12 @@
             tiles = [lambda k: row_of(3, k, 0)]
         return [[tile(k) for k in range(5)] for tile in tiles]
 
+    def write_smoothed(g, carry):
+        at, rows = pl.ds(XO + 4 * g, 4), pl.ds(YO, 64)
+        moved = permuted(ping0[0, at, rows, :], ping0[1, at, rows, :], back[...])
+        sm[pl.ds(4 * g, 4)] = moved.reshape(4, 64, 256)
+        return carry
+
     for n, level in enumerate(LEVELS):
         raw, ext, packed, received, halved = raws[n], exts[n], packs[n], receiveds[n], halveds[n]
         if n > 0:
@@ -489,35 +608,38 @@
                 )
                 copies[offset].start()
             pending += list(copies.values())
+        ping, pong = pings[n], pongs[n]
+        if n == 1:
+            coarser_constants()
         coefs = level_coefs(n)
-        for c in copies.values():
-            c.wait_recv()
-        begin(level, raw, received, ext, coefs)
-        relax(level, ext, pings[n], pongs[n], coefs)
         if n == 0:
-            stores = [
-                pltpu.make_async_copy(
-                    ping0.at[t, pl.ds(XO, 16), pl.ds(YO, 64), :],
-                    smooth_ref.at[:, :, pl.ds(LANES * t, LANES)],
-                    local.at[2 + t],
-                )
-                for t in range(2)
-            ]
-            for c in stores:
-                c.start()
+            for offset, c in copies.items():
+                if offset[0] == 0:
+                    c.wait_recv()
+            begin(level, raw, received, ext, coefs, ("own",))
+            relax(level, ext, ping, pong, coefs, 0)
+            for offset, c in copies.items():
+                if offset[0] != 0:
+                    c.wait_recv()
+            begin(level, raw, received, ext, coefs, ("halo",))
+            relax_wings(level, ext, ping, pong, coefs)
+        else:
+            if n == 1:
+                lax.fori_loop(0, 4, write_smoothed, 0)
+                stores = [pltpu.make_async_copy(sm, smooth_ref, local.at[2])]
+                stores[0].start()
+            for c in copies.values():
+                c.wait_recv()
+            begin(level, raw, received, ext, coefs, ("own", "halo"))
+            relax(level, ext, ping, pong, coefs, HALO)
         residual_rows(level, ext, pings[n], coefs, pair, halved)
-        if n == 0:
-            total = select_dot(halved[0].reshape(256, LANES), halving(0, 0.5)) + select_dot(
-                halved[1].reshape(256, LANES), halving(64, 0.5)
-            )
-            raw1[0] = total.reshape(8, 32, LANES)
-        elif n == 1:
-            raw2[0] = select_dot(halved[0].reshape(64, LANES), halving(0, 0.5)).reshape(
+        if n == 1:
+            raw2[0] = select_dot(halved[0].reshape(64, LANES), halving(0, 1.0)).reshape(
                 4, 16, LANES
             )
-        else:
+        elif n == 2:
             k = lax.broadcasted_iota(jnp.int32, (LANES, LANES), 0)
-            picks = jnp.where(k < 64, halving(32 * gz, 0.5), 0.0)
+            picks = jnp.where(k < 64, halving(32 * gz, 1.0), 0.0)
             column[gz] = select_dot(halved[0].reshape(16, LANES), picks).reshape(2, 8, LANES)
 
     copies = [remote(column.at[gz], column.at[gz], offset) for offset in PROFILE_PEERS]
@@ -558,7 +680,17 @@
     coarse_ref[...] = ping3[0, pl.ds(8, 2), pl.ds(8, 32), :]
     for c in copies:
         c.wait_send()
-    for c in stores:
+    stores[0].wait()
+
+
+def hand_out(smoothed, coarse, smooth_out, coarse_out, sems):
+    copies = [
+        pltpu.make_async_copy(smoothed, smooth_out, sems.at[0]),
+        pltpu.make_async_copy(coarse, coarse_out, sems.at[1]),
+    ]
+    for c in copies:
+        c.start()
+    for c in copies:
         c.wait()
 
 
@@ -568,7 +700,7 @@
     vmem = pl.BlockSpec(memory_space=pltpu.VMEM)
     hbm = pl.BlockSpec(memory_space=pltpu.HBM)
     tile = (8, LANES)
-    return pl.pallas_call(
+    smoothed, coarse = pl.pallas_call(
         kernel,
         out_shape=(
             jax.ShapeDtypeStruct((16, 64, 256), f32),
@@ -584,6 +716,10 @@
             pltpu.VMEM(LEVELS[1]["shape"], f32),
             pltpu.VMEM(LEVELS[2]["shape"], f32),
             pltpu.VMEM((1, 18, 48, LANES), f32),
+            pltpu.VMEM((2, 16, 64, LANES), f32),
+            pltpu.VMEM((16, 64, 256), f32),
+            pltpu.VMEM((256, 256), jnp.bfloat16),
+            pltpu.VMEM((256, 256), jnp.bfloat16),
             pltpu.VMEM(LEVELS[0]["shape"], f32),
             pltpu.VMEM(LEVELS[1]["shape"], f32),
             pltpu.VMEM(LEVELS[2]["shape"], f32),
@@ -601,10 +737,10 @@
             pltpu.VMEM((2, 256), f32),
             pltpu.VMEM((4,) + tile, f32),
             pltpu.VMEM((2,) + tile, f32),
-            pltpu.VMEM((3, 16, LANES), f32),
+            pltpu.VMEM((3, 2, 16, LANES), f32),
             pltpu.VMEM((4, 5) + tile, f32),
-            pltpu.VMEM((2, 64, LANES), f32),
-            pltpu.VMEM((2, 8, 32, LANES), f32),
+            pltpu.VMEM((2, 5) + tile, f32),
+            pltpu.VMEM((64, LANES), f32),
             pltpu.VMEM((1, 4, 16, LANES), f32),
             pltpu.VMEM((1, 2, 8, LANES), f32),
             pltpu.VMEM((4, 2) + tile, f32),
@@ -615,9 +751,10 @@
             pltpu.SemaphoreType.REGULAR((2,)),
         ],
         compiler_params=pltpu.CompilerParams(
-            collective_id=0, has_side_effects=True, vmem_limit_bytes=62 << 20
+            collective_id=0, has_side_effects=True, vmem_limit_bytes=52 << 20
         ),
     )(source, cell, face)
+    return smoothed, coarse
 
 
 def solution(mesh):

time: 69.6 us -> 64.5 us (0.927)
  Pallas kernels: 65.9 us -> 60.8 us
    pallas_call x1, Pallas kernels: 65.9 us -> 60.8 us  [on_device(): pl.pallas_call(kernel, out_shape=(jax.ShapeDtypeStruct((16, 64, 256), f32...]
    unnamed x4 -> x6, local copies, waits for them, and re-layouts: 2.92 us -> 2.94 us
where the time goes in v4:
time: 64.5 us; the launch traced here: 64.4 us
  Pallas kernels  60.8 us (94%)
  local copies, waits for them, and re-layouts  2.94 us (5%)
  between operations  0.65 us (1%)
    pallas_call x1, Pallas kernels, on_device(): pl.pallas_call(kernel, out_shape=(jax.ShapeDtypeStruct((16, 64, 256), f32...  60.8 us
    unnamed x6, local copies, waits for them, and re-layouts  2.94 us

profile of v4, /device:TPU:1, one launch (start us, length us, event | category | flops | bytes accessed | tf_op | source)
XLA Modules:
  0.0 64.4 jit_solution(8560297249542194591)
XLA Ops:
  0.6 0.0 copy-start
  0.6 0.7 %copy-done = f32[256]{0:T(256)S(1)} copy-done((f32[256]{0:T(256)S(1)}, f32[256]{0:T(256)}, u32[]{:S(2)}) %copy-start) | copy-done | bytes 1048
  1.3 0.0 copy-start.1
  1.3 0.7 %copy-done.1 = f32[256]{0:T(256)S(1)} copy-done((f32[256]{0:T(256)S(1)}, f32[256]{0:T(256)}, u32[]{:S(2)}) %copy-start.1) | copy-done | bytes 1048
  2.0 60.8 %shard_map.50 = (f32[16,64,256]{2,1,0:T(8,128)S(1)}, f32[2,32,128]{2,1,0:T(8,128)S(1)}) custom-call(f32[16,64,256]{2,1,0:T(8,128)} %source_ref.1, f32[256]{0:T(256)S(1)} %copy-done, f32[256]{0:T(256)S(1)} %copy-done.1), custom_call_target="tpu_custom_call" | custom-call | tf_op jit(solution)/shard_map/pallas_call | solution.py:703
  62.8 1.0 %copy.7 = f32[16,64,256]{2,1,0:T(8,128)} copy(f32[16,64,256]{2,1,0:T(8,128)S(1)} %get-tuple-element.4) | data formatting | bytes 2097152
  63.7 0.6 copy.8
Async XLA Ops:
  0.6 0.7 %copy-start = (f32[256]{0:T(256)S(1)}, f32[256]{0:T(256)}, u32[]{:S(2)}) copy-start(f32[256]{0:T(256)} %cell_ref.1) | copy-start | bytes 3076
  1.3 0.7 %copy-start.1 = (f32[256]{0:T(256)S(1)}, f32[256]{0:T(256)}, u32[]{:S(2)}) copy-start(f32[256]{0:T(256)} %face_ref.1) | copy-start | bytes 3076

commit v5 on v4

--- a/solution.py
+++ b/solution.py
@@ -295,21 +295,19 @@
 
 def begin(level, raw, received, ext, coefs, parts):
     tiles, own, nx, block = level["tiles"], level["own"], level["x"], level["block"]
-    strips, step = level["y"] // 8 + 2, max(level["step"], 2)
+    strips, blocks = level["y"] // 8 + 2, nx // block
     lane = lane_iota()
     even = lax.rem(lane // 8, 2) == 0
     base = 64 if tiles == 1 else 0
 
-    def halo_tile(x, j):
-        e, i = x // block, lax.rem(x, block)
-        both = jnp.where(even, received[1, e, j], received[0, e, j])
-        return pltpu.roll(both, lax.rem(base + LANES - 16 * i, LANES), 1)
-
-    def plane_of(inside):
-        def plane(x):
-            for j in range(strips):
-                row = 8 + 8 * j
-                ends = halo_tile(x, j)
+    def planes_of(e, planes, inside):
+        for j in range(strips):
+            row = 8 + 8 * j
+            both = jnp.where(even, received[1, e, j], received[0, e, j])
+            for i in planes:
+                x = e * block + i
+                shift = (base + LANES - 16 * i) % LANES
+                ends = pltpu.roll(both, shift, 1) if shift else both
                 for t in range(own):
                     if inside and 0 < j < strips - 1:
                         b = raw[t, x - XO, pl.ds(8 * (j - 1), 8), :]
@@ -321,23 +319,27 @@
                 if tiles > 1:
                     ext[own, x, pl.ds(row, 8), :] = ends * coefs[own][3]
 
-        def some(x):
-            for k in range(step):
-                plane(x + k)
-
-        return some
-
+    first = XO // block
     if "own" in parts:
-        for_each(XO, XO + nx, step, plane_of(True))
+        if blocks == 1:
+            planes_of(first, range(block), True)
+        else:
+
+            def turn(e, carry):
+                planes_of(e, range(block), True)
+                return carry
+
+            lax.fori_loop(first, first + blocks, turn, 0)
     if "halo" in parts:
-        for_each(XO - HALO, XO, step, plane_of(False))
-        for_each(XO + nx, XO + nx + HALO, step, plane_of(False))
+        for e in list(range(first)) + list(range(first + blocks, first + blocks + XO // block)):
+            planes = [i for i in range(block) if XO - HALO <= e * block + i < XO + nx + HALO]
+            planes_of(e, planes, False)
 
 
 def residual_rows(level, ext, ping, coefs, pair, halved):
     tiles, own, nx, ny = level["tiles"], level["own"], level["x"], level["y"]
 
-    def planes(p, carry):
+    def planes(p):
         for j in range(ny // 8):
             row = YO + 8 * j
             total = [None] * own
@@ -351,13 +353,19 @@
             row_sum = total[0] * coefs[0][4]
             if own == 2:
                 row_sum = row_sum + total[1] * coefs[1][4]
-            pair[pl.ds(8 * j, 8), :] = row_sum
+            pair[p, pl.ds(8 * j, 8), :] = row_sum
+
+    def rows(p):
         halved[0, p] = 0.5 * (
-            pair[pl.ds(0, ny // 2, stride=2), :] + pair[pl.ds(1, ny // 2, stride=2), :]
+            pair[p, pl.ds(0, ny // 2, stride=2), :] + pair[p, pl.ds(1, ny // 2, stride=2), :]
         )
-        return carry
-
-    lax.fori_loop(0, nx // 2, planes, 0)
+
+    for body in (planes, rows):
+        if own == 2:
+            for_each(0, nx // 2, 1, body)
+        else:
+            for p in range(nx // 2):
+                body(p)
 
 
 def kernel(
@@ -429,7 +437,7 @@
     halveds = (raw1, halved1, halved2)
 
     barrier = pltpu.get_barrier_semaphore()
-    peers = FACES + ((0, 0, 2),)
+    peers = FACES + ((0, 0, 2), (0, 1, 1), (0, 1, -1), (0, -1, 1), (0, -1, -1))
     for offset in peers:
         pl.semaphore_signal(
             barrier, inc=1, device_id=device_at(place, offset), device_id_type=MESH
@@ -475,8 +483,9 @@
     profiles = [remote(mine, mine, offset) for offset in PROFILE_PEERS]
     for c in profiles:
         c.start()
-    for offset in FACES[:1:-1]:
-        copies[offset].start()
+    for offset in peers[:1:-1]:
+        if offset in copies:
+            copies[offset].start()
     for stage, distance in ((0, 2), (1, 3)):
         for offset in FACES:
             pl.semaphore_signal(
@@ -484,6 +493,8 @@
             )
         pl.semaphore_wait(greet.at[stage], len(FACES))
         for offset in sorted(copies, key=lambda o: abs(o[0])):
+            if offset in peers[2:]:
+                continue
             if sum(abs(o) for o in offset) == distance:
                 copies[offset].start()
             elif distance == 2 and offset in FACES[:2]:
@@ -601,7 +612,7 @@
         if n > 0:
             pack_faces(level, raw, packed)
             copies = {}
-            order = sorted(offsets_of(level), key=lambda o: -sum(abs(i) for i in o))
+            order = sorted(offsets_of(level), key=lambda o: (abs(o[2])==0, -sum(abs(i) for i in o)))
             for offset in order:
                 copies[offset] = remote(
                     *message(level, raw, packed, ext, received, offset), offset
@@ -740,7 +751,7 @@
             pltpu.VMEM((3, 2, 16, LANES), f32),
             pltpu.VMEM((4, 5) + tile, f32),
             pltpu.VMEM((2, 5) + tile, f32),
-            pltpu.VMEM((64, LANES), f32),
+            pltpu.VMEM((8, 64, LANES), f32),
             pltpu.VMEM((1, 4, 16, LANES), f32),
             pltpu.VMEM((1, 2, 8, LANES), f32),
             pltpu.VMEM((4, 2) + tile, f32),

time: 64.5 us -> 60.5 us (0.938)
  Pallas kernels: 60.8 us -> 56.7 us
    pallas_call x1, Pallas kernels: 60.8 us -> 56.7 us  [on_device(): pl.pallas_call(kernel, out_shape=(jax.ShapeDtypeStruct((16, 64, 256), f32...]
where the time goes in v5:
time: 60.5 us; the launch traced here: 60.3 us
  Pallas kernels  56.7 us (94%)
  local copies, waits for them, and re-layouts  2.94 us (5%)
  between operations  0.65 us (1%)
    pallas_call x1, Pallas kernels, on_device(): pl.pallas_call(kernel, out_shape=(jax.ShapeDtypeStruct((16, 64, 256), f32...  56.7 us
    unnamed x6, local copies, waits for them, and re-layouts  2.94 us

profile of v5, /device:TPU:1, one launch (start us, length us, event | category | flops | bytes accessed | tf_op | source)
XLA Modules:
  0.0 60.3 jit_solution(5190602938660059527)
XLA Ops:
  0.6 0.0 copy-start
  0.6 0.7 %copy-done = f32[256]{0:T(256)S(1)} copy-done((f32[256]{0:T(256)S(1)}, f32[256]{0:T(256)}, u32[]{:S(2)}) %copy-start) | copy-done | bytes 1048
  1.3 0.0 copy-start.1
  1.3 0.7 %copy-done.1 = f32[256]{0:T(256)S(1)} copy-done((f32[256]{0:T(256)S(1)}, f32[256]{0:T(256)}, u32[]{:S(2)}) %copy-start.1) | copy-done | bytes 1048
  2.0 56.7 %shard_map.50 = (f32[16,64,256]{2,1,0:T(8,128)S(1)}, f32[2,32,128]{2,1,0:T(8,128)S(1)}) custom-call(f32[16,64,256]{2,1,0:T(8,128)} %source_ref.1, f32[256]{0:T(256)S(1)} %copy-done, f32[256]{0:T(256)S(1)} %copy-done.1), custom_call_target="tpu_custom_call" | custom-call | tf_op jit(solution)/shard_map/pallas_call | solution.py:714
  58.7 1.0 %copy.7 = f32[16,64,256]{2,1,0:T(8,128)} copy(f32[16,64,256]{2,1,0:T(8,128)S(1)} %get-tuple-element.4) | data formatting | bytes 2097152
  59.7 0.6 %copy.8 = f32[2,32,128]{2,1,0:T(8,128)} copy(f32[2,32,128]{2,1,0:T(8,128)S(1)} %get-tuple-element.5) | data formatting | bytes 65536
Async XLA Ops:
  0.6 0.7 %copy-start = (f32[256]{0:T(256)S(1)}, f32[256]{0:T(256)}, u32[]{:S(2)}) copy-start(f32[256]{0:T(256)} %cell_ref.1) | copy-start | bytes 3076
  1.3 0.7 %copy-start.1 = (f32[256]{0:T(256)S(1)}, f32[256]{0:T(256)}, u32[]{:S(2)}) copy-start(f32[256]{0:T(256)} %face_ref.1) | copy-start | bytes 3076

commit v6 on v5

--- a/solution.py
+++ b/solution.py
@@ -18,7 +18,7 @@
 
 LEVELS = (
     dict(x=16, y=64, own=2, split=True, tiles=3, block=8, reach=1, step=1, shape=(3, 32, 96, LANES)),
-    dict(x=8, y=32, own=1, split=False, tiles=2, block=8, reach=1, step=2, shape=(2, 24, 64, LANES)),
+    dict(x=8, y=32, own=1, split=False, tiles=2, block=8, reach=1, step=0, shape=(2, 24, 64, LANES)),
     dict(x=4, y=16, own=1, split=False, tiles=1, block=4, reach=2, step=0, shape=(1, 20, 48, LANES)),
 )
 
@@ -281,7 +281,7 @@
 
     def both(s, source, target):
         for first in (XO - HALO + s, XO + nx - s):
-            update(tiles, ext, source, target, first, first + HALO, 1, strips, coefs, finish)
+            update(tiles, ext, source, target, first, first + HALO, 3, strips, coefs, finish)
 
     both(1, ext, ping)
 

time: 60.5 us -> 55.2 us (0.912)
  Pallas kernels: 56.7 us -> 51.5 us
    pallas_call x1, Pallas kernels: 56.7 us -> 51.5 us  [on_device(): pl.pallas_call(kernel, out_shape=(jax.ShapeDtypeStruct((16, 64, 256), f32...]
where the time goes in v6:
time: 55.2 us; the launch traced here: 55.1 us
  Pallas kernels  51.5 us (93%)
  local copies, waits for them, and re-layouts  2.94 us (5%)
  between operations  0.65 us (1%)
    pallas_call x1, Pallas kernels, on_device(): pl.pallas_call(kernel, out_shape=(jax.ShapeDtypeStruct((16, 64, 256), f32...  51.5 us
    unnamed x6, local copies, waits for them, and re-layouts  2.94 us

profile of v6, /device:TPU:1, one launch (start us, length us, event | category | flops | bytes accessed | tf_op | source)
XLA Modules:
  0.0 55.1 jit_solution(11220377157531728395)
XLA Ops:
  0.6 0.0 copy-start
  0.6 0.7 %copy-done = f32[256]{0:T(256)S(1)} copy-done((f32[256]{0:T(256)S(1)}, f32[256]{0:T(256)}, u32[]{:S(2)}) %copy-start) | copy-done | bytes 1048
  1.3 0.0 copy-start.1
  1.3 0.7 %copy-done.1 = f32[256]{0:T(256)S(1)} copy-done((f32[256]{0:T(256)S(1)}, f32[256]{0:T(256)}, u32[]{:S(2)}) %copy-start.1) | copy-done | bytes 1048
  2.0 51.5 %shard_map.50 = (f32[16,64,256]{2,1,0:T(8,128)S(1)}, f32[2,32,128]{2,1,0:T(8,128)S(1)}) custom-call(f32[16,64,256]{2,1,0:T(8,128)} %source_ref.1, f32[256]{0:T(256)S(1)} %copy-done, f32[256]{0:T(256)S(1)} %copy-done.1), custom_call_target="tpu_custom_call" | custom-call | tf_op jit(solution)/shard_map/pallas_call | solution.py:714
  53.5 1.0 %copy.7 = f32[16,64,256]{2,1,0:T(8,128)} copy(f32[16,64,256]{2,1,0:T(8,128)S(1)} %get-tuple-element.4) | data formatting | bytes 2097152
  54.5 0.6 %copy.8 = f32[2,32,128]{2,1,0:T(8,128)} copy(f32[2,32,128]{2,1,0:T(8,128)S(1)} %get-tuple-element.5) | data formatting | bytes 65536
Async XLA Ops:
  0.6 0.7 %copy-start = (f32[256]{0:T(256)S(1)}, f32[256]{0:T(256)}, u32[]{:S(2)}) copy-start(f32[256]{0:T(256)} %cell_ref.1) | copy-start | bytes 3076
  1.3 0.7 %copy-start.1 = (f32[256]{0:T(256)S(1)}, f32[256]{0:T(256)}, u32[]{:S(2)}) copy-start(f32[256]{0:T(256)} %face_ref.1) | copy-start | bytes 3076
